TPU v7x, 256 devices: a whole 4x4x8 slice. The times are simulated.
256 devices in a mesh: dp: 4 (over x_hi, core), latent: 64 (over y, x_lo, z).
Axes of the slice: x: 4 (x_hi: 2, x_lo: 2; x = x_hi * 2 + x_lo), y: 4, z: 8, core: 2. Of those that a mesh axis runs over, the one named last changes fastest.
Arguments:
- activations: bfloat16 [32768, 8192], P(('dp', 'latent')), may hold values from -6 to 6
- owner_ids: int32 [32768, 2], P(('dp', 'latent')), may hold values from 0 to 63, all different within a row; in each aligned block of 128 rows (0 to 127, 128 to 255, ...) at most 6 rows name the same one
- block_mask: int32 [32768, 2, 8], P(('dp', 'latent')), may hold values 0 or 1
- latent_codes: bfloat16 [32768, 2, 1024], P(('dp', 'latent')), may hold values from 0.099609375 to 4
- w_dec: bfloat16 [65536, 8192], P('latent', 'dp'), may hold values from -0.125 to 0.125
- b_dec: float32 [8192], replicated, may hold values from -3 to 3
Outputs:
- rebuilt: bfloat16 [32768, 8192], P(('dp', 'latent'))
- decoder_grad: bfloat16 [65536, 8192], P('latent', 'dp')
Inputs may be any that keep to these rules, and one draw needn't show every extreme that they name: `owner_ids`: each row names 2 different owners; among the rows of one device no owner is named more than 6 times, and in every draw some device names some owner exactly 6 times.
All inputs are finite; a program needn't handle non-finite values. No bound on the sum of `block_mask` on one device may be relied on, other than what follows from the above.
Results may differ from a plain program's by a relative error of at most 0.0047.
Values may be sent and summed in bfloat16 or wider, within the bound.
A program may use at most 128 MiB of HBM per device.

v0:
```python
import jax
import jax.numpy as jnp
from jax import lax
from jax.sharding import PartitionSpec as P

loss_scale = 1.0 / 32.0


def on_device(activations, owner_ids, block_mask, latent_codes, w_dec, b_dec):
    row_count, visit_count = owner_ids.shape
    block_count = block_mask.shape[2]
    slab_width = latent_codes.shape[2]
    block_width = slab_width // block_count
    model_width = activations.shape[1]
    owners = lax.axis_size("latent")
    groups = lax.axis_size("dp")
    capacity = row_count * visit_count // owners + 2
    live = block_mask.astype(latent_codes.dtype)[:, :, :, None]
    used = (latent_codes.reshape(row_count, visit_count, block_count, block_width) * live).reshape(
        -1, slab_width
    )
    onehot = (owner_ids[:, :, None] == lax.broadcasted_iota(jnp.int32, (1, 1, owners), 2)).astype(
        jnp.int32
    )
    per_row = jnp.sum(onehot, axis=1)
    before = jnp.cumsum(per_row, axis=0) - per_row
    position = jnp.sum(onehot * before[:, None, :], axis=2)
    target_slot = (owner_ids * capacity + position).reshape(-1)
    outgoing = jnp.zeros((owners * capacity, slab_width), latent_codes.dtype)
    outgoing = outgoing.at[target_slot].set(used).reshape(owners, capacity, slab_width)
    arrived = lax.all_to_all(outgoing, "latent", split_axis=0, concat_axis=0, tiled=True)
    copies = lax.all_gather(arrived, "dp", axis=0, tiled=True)
    arrived_flat = arrived.reshape(owners * capacity, slab_width)
    decoded = jnp.dot(
        arrived_flat,
        lax.all_gather(w_dec, "dp", axis=1, tiled=True),
        preferred_element_type=jnp.float32,
    ).astype(jnp.bfloat16)
    returned = lax.all_to_all(
        decoded.reshape(owners, capacity, model_width),
        "latent",
        split_axis=0,
        concat_axis=0,
        tiled=True,
    )
    returned = returned.reshape(owners * capacity, model_width)
    gathered = returned[target_slot].reshape(row_count, visit_count, model_width)
    rebuilt_wide = b_dec[None, :] + jnp.sum(gathered, axis=1, dtype=jnp.float32)
    errors = (rebuilt_wide - activations.astype(jnp.float32)).astype(jnp.bfloat16)
    error_slots = jnp.zeros((owners * capacity, model_width), jnp.bfloat16)
    error_slots = error_slots.at[target_slot].set(jnp.repeat(errors, visit_count, axis=0))
    error_slots = error_slots.reshape(1, owners, capacity, model_width)
    error_parts = lax.all_to_all(
        lax.all_to_all(error_slots, "dp", split_axis=3, concat_axis=0, tiled=True),
        "latent",
        split_axis=1,
        concat_axis=1,
        tiled=True,
    )
    error_parts = error_parts.reshape(groups * owners, capacity, error_parts.shape[3])
    gradient = (
        jnp.einsum("nsi,nsd->id", copies, error_parts, preferred_element_type=jnp.float32)
        * loss_scale
    )
    return (rebuilt_wide.astype(jnp.bfloat16), gradient.astype(jnp.bfloat16))


def solution(mesh):
    placed = (
        P(("dp", "latent"), None),
        P(("dp", "latent"), None),
        P(("dp", "latent"), None, None),
        P(("dp", "latent"), None, None),
        P("latent", "dp"),
        P(),
    )
    return jax.shard_map(
        on_device,
        mesh=mesh,
        in_specs=placed,
        out_specs=(P(("dp", "latent"), None), P("latent", "dp")),
        check_vma=False,
    )
```

profile of v0, /device:TPU:1, one launch (start us, length us, event | category | flops | bytes accessed | tf_op | source)
XLA Modules:
  0.0 756.3 jit_solution(3397413485962751764)
XLA Ops:
  7.2 0.7 all-gather.3.cloned.1.call-update
  7.9 0.7 convert_reduce_fusion
  8.9 0.7 select_reduce_fusion
  9.7 0.7 multiply_add_fusion
  10.6 0.7 convert_element_type.28
  11.4 1.2 reshape.78
  13.0 1.9 scatter_custom_fusion
  15.3 39.9 %all_to_all.33 = bf16[64,6,1024]{2,1,0:T(8,128)(2,1)S(1)} all-to-all(bf16[64,6,1024]{2,1,0:T(8,128)(2,1)S(1)} %reshape.79), channel_id=1, replica_groups=mesh['dp'=4,'latent'=64] {'latent'}, dimensions={0} | all-to-all | bytes 1572864 | tf_op jit(solution)/shard_map/all_to_all | solution.py:31
  55.4 80.7 %all-gather.3.cloned.1.call-done = bf16[1024,8192]{1,0:T(8,128)(2,1)} async-done(((bf16[1024,2048]{1,0:T(8,128)(2,1)}), bf16[1024,8192]{1,0:T(8,128)(2,1)}) %all-gather.3.cloned.1.call-update) | async-done | bytes 16777232 | tf_op jit(solution)/shard_map/all_gather | solution.py:36
  136.1 14.4 %convolution_convert_fusion = bf16[384,8192]{1,0:T(8,128)(2,1)} fusion(bf16[384,1024]{1,0:T(8,128)(2,1)S(1)} %reshape.80, bf16[1024,8192]{1,0:T(8,128)(2,1)} %all-gather.3.cloned.1.call-done), kind=kOutput, calls=%fused_computation.3 | convolution fusion | flops 6445596672 | bytes 23855104 | tf_op jit(solution)/shard_map/dot_general | solution.py:34
  150.5 8.9 %reshape.81 = bf16[64,6,8192]{2,1,0:T(8,128)(2,1)} reshape(bf16[384,8192]{1,0:T(8,128)(2,1)} %convolution_convert_fusion) | data formatting | bytes 12582912 | tf_op jit(solution)/shard_map/reshape | solution.py:40
  159.4 10.5 %all-to-all-start.1 = ((bf16[64,6,8192]{2,1,0:T(8,128)(2,1)}), bf16[64,6,8192]{2,1,0:T(8,128)(2,1)}, u32[]{:S(2)}, u32[]{:S(2)}) async-start(bf16[64,6,8192]{2,1,0:T(8,128)(2,1)} %reshape.81), calls=%async_computation.1 | async-start | bytes 16777216 | tf_op jit(solution)/shard_map/all_to_all | solution.py:39
  170.0 182.0 %all-to-all-done.1 = bf16[64,6,8192]{2,1,0:T(8,128)(2,1)} async-done(((bf16[64,6,8192]{2,1,0:T(8,128)(2,1)}), bf16[64,6,8192]{2,1,0:T(8,128)(2,1)}, u32[]{:S(2)}, u32[]{:S(2)}) %all-to-all-start.1) | async-done | bytes 6291488 | tf_op jit(solution)/shard_map/all_to_all | solution.py:39
  352.0 9.1 %reshape.82 = bf16[384,8192]{1,0:T(8,128)(2,1)} reshape(bf16[64,6,8192]{2,1,0:T(8,128)(2,1)} %all-to-all-done.1) | data formatting | bytes 12582912 | tf_op jit(solution)/shard_map/reshape | solution.py:46
  361.1 12.6 %gather_fusion = bf16[256,8192]{1,0:T(8,128)(2,1)} fusion(bf16[384,8192]{1,0:T(8,128)(2,1)} %reshape.82, s32[1024]{0:T(1024)S(1)} %pad_clamp_fusion), kind=kCustom, calls=%fused_computation | custom fusion | bytes 8389632 | tf_op jit(solution)/shard_map/gather | solution.py:47
  373.7 9.7 %reshape.86 = f32[128,2,8192]{2,1,0:T(2,128)} reshape(bf16[256,8192]{1,0:T(8,128)(2,1)} %gather_fusion) | data formatting | bytes 12582912 | tf_op jit(solution)/shard_map/convert_element_type | solution.py:48
  383.3 13.5 %reduce_sum.29 = f32[128,8192]{1,0:T(8,128)} reduce(f32[128,2,8192]{2,1,0:T(2,128)} %reshape.86, f32[]{:T(128)} %constant.4.clone.1), dimensions={1}, to_apply=%region_4.5 | reduce | flops 1048576 | bytes 12582916 | tf_op jit(solution)/shard_map/reduce_sum | solution.py:48
  396.9 4.1 subtract_convert_fusion
  401.0 4.1 broadcast_in_dim.8
  405.1 7.4 reshape.107
  412.5 11.3 %scatter_custom_fusion.1 = bf16[384,8192]{1,0:T(8,128)(2,1)} fusion(s32[256]{0:T(256)S(1)} %bitcast.28, bf16[256,8192]{1,0:T(8,128)(2,1)} %reshape.107, bf16[]{:T(256)} %constant.6.clone.1), kind=kCustom, calls=%fused_computation.8 | custom fusion | bytes 6291968 | tf_op jit(solution)/shard_map/scatter | solution.py:51
  423.7 9.1 %reshape.84 = bf16[1,64,6,8192]{3,2,1,0:T(8,128)(2,1)} reshape(bf16[384,8192]{1,0:T(8,128)(2,1)} %scatter_custom_fusion.1) | data formatting | bytes 12582912 | tf_op jit(solution)/shard_map/reshape | solution.py:52
  432.8 21.9 %copy.39 = bf16[1,64,6,8192]{1,2,0,3:T(8,128)(2,1)} copy(bf16[1,64,6,8192]{3,2,1,0:T(8,128)(2,1)} %reshape.84) | data formatting | bytes 12582912 | tf_op jit(solution)/shard_map/reshape | solution.py:52
  454.7 14.3 %reshape.116 = bf16[4,2,393216]{2,1,0:T(2,128)(2,1)} reshape(bf16[8192,1,6,64]{3,2,1,0:T(8,128)(2,1)} %bitcast.21) | data formatting | bytes 12582912
  468.9 79.5 %all_to_all.34 = bf16[4,2,393216]{2,1,0:T(2,128)(2,1)} all-to-all(bf16[4,2,393216]{2,1,0:T(2,128)(2,1)} %reshape.116), channel_id=1, replica_groups=mesh['dp'=4,'latent'=64] {'dp'}, dimensions={0} | all-to-all | bytes 12582912 | tf_op jit(solution)/shard_map/all_to_all | solution.py:54
  548.4 13.5 %reshape.117 = bf16[8192,1,6,64]{3,2,1,0:T(8,128)(2,1)} reshape(bf16[4,2,393216]{2,1,0:T(2,128)(2,1)} %all_to_all.34) | data formatting | bytes 12582912
  561.9 17.9 %copy.44 = bf16[1,64,6,4,2048]{4,3,2,1,0:T(4,128)(2,1)} copy(bf16[1,64,6,4,2048]{1,2,4,3,0:T(8,128)(2,1)} %bitcast.22) | data formatting | bytes 12582912 | tf_op jit(solution)/shard_map/all_to_all | solution.py:54
  579.7 13.0 %all-to-all-start.3 = ((bf16[4,64,6,2048]{3,0,2,1:T(4,128)(2,1)}), bf16[4,64,6,2048]{3,0,2,1:T(4,128)(2,1)}, u32[]{:S(2)}, u32[]{:S(2)}) async-start(bf16[4,64,6,2048]{3,0,2,1:T(4,128)(2,1)} %bitcast.23), calls=%async_computation.3 | async-start | bytes 12582912 | tf_op jit(solution)/shard_map/all_to_all | solution.py:53
  593.1 1.3 copy.38
  594.4 134.6 %all-to-all-done.3 = bf16[4,64,6,2048]{3,0,2,1:T(4,128)(2,1)} async-done(((bf16[4,64,6,2048]{3,0,2,1:T(4,128)(2,1)}), bf16[4,64,6,2048]{3,0,2,1:T(4,128)(2,1)}, u32[]{:S(2)}, u32[]{:S(2)}) %all-to-all-start.3) | async-done | bytes 6291488 | tf_op jit(solution)/shard_map/all_to_all | solution.py:53
  729.0 9.0 %copy.42 = bf16[4,64,6,2048]{3,1,0,2:T(8,128)(2,1)} copy(bf16[4,64,6,2048]{3,0,2,1:T(4,128)(2,1)} %all-to-all-done.3) | data formatting | bytes 12582912 | tf_op jit(solution)/shard_map/all_to_all | solution.py:53
  738.0 11.2 %fusion = bf16[1024,2048]{1,0:T(8,128)(2,1)} fusion(bf16[256,6,1024]{2,0,1:T(8,128)(2,1)} %all-gather.5.cloned.1.call-done, bf16[256,6,2048]{2,0,1:T(8,128)(2,1)} %bitcast.24), kind=kOutput, calls=%fused_computation.5 | convolution fusion | flops 6446645248 | bytes 13631488 | tf_op jit(solution)/shard_map/nsi,nsd->id/dot_general | solution.py:62
  (20 shorter events, 1.9 us)
Async XLA Ops:
  7.2 129.0 %all-gather.3.cloned.1.call-start = ((), (), s32[]{:S(2)}) async-start(), calls=%async_computation.4 | async-start | bytes 20971520 | tf_op jit(solution)/shard_map/all_gather | solution.py:36
  159.4 192.5 %all-to-all-start.1 = ((bf16[64,6,8192]{2,1,0:T(8,128)(2,1)}), bf16[64,6,8192]{2,1,0:T(8,128)(2,1)}, u32[]{:S(2)}, u32[]{:S(2)}) async-start(bf16[64,6,8192]{2,1,0:T(8,128)(2,1)} %reshape.81), calls=%async_computation.1 | async-start | bytes 16777216 | tf_op jit(solution)/shard_map/all_to_all | solution.py:39
  383.3 13.5 %copy-start = (bf16[128,8192]{1,0:T(8,128)(2,1)S(1)}, bf16[128,8192]{1,0:T(8,128)(2,1)}, u32[]{:S(2)}) copy-start(bf16[128,8192]{1,0:T(8,128)(2,1)} %param.6) | copy-start | bytes 6291460
  383.3 13.5 %copy-start.1 = (f32[8192]{0:T(1024)S(1)}, f32[8192]{0:T(1024)}, u32[]{:S(2)}) copy-start(f32[8192]{0:T(1024)} %param.11) | copy-start | bytes 98308
  579.7 149.2 %all-to-all-start.3 = ((bf16[4,64,6,2048]{3,0,2,1:T(4,128)(2,1)}), bf16[4,64,6,2048]{3,0,2,1:T(4,128)(2,1)}, u32[]{:S(2)}, u32[]{:S(2)}) async-start(bf16[4,64,6,2048]{3,0,2,1:T(4,128)(2,1)} %bitcast.23), calls=%async_computation.3 | async-start | bytes 12582912 | tf_op jit(solution)/shard_map/all_to_all | solution.py:53
  592.8 145.2 %all-gather.5.cloned.1.call-start = ((), (), s32[]{:S(2)}) async-start(), calls=%async_computation.5 | async-start | bytes 3932160 | tf_op jit(solution)/shard_map/all_gather | solution.py:32
Sparse Core Ops, SparseCore 0:
  9.8 126.2 all-gather.2
  596.0 45.9 all-gather.4
where the time goes:
time: 769 us; the launch traced here: 756 us
  waiting for transfers between devices  398 us (52%)
  local copies, waits for them, and re-layouts  153 us (20%)
  blocking collectives  119 us (15%)
  matrix products  25.5 us (3%)
  starting transfers between devices  23.9 us (3%)
  other arithmetic  22.6 us (3%)
  between operations  14.4 us (2%)
    all_to_all x1, waiting for transfers between devices, on_device(): lax.all_to_all(decoded.reshape(owners, capacity, model_width), 'latent',...  182 us
    all_to_all x1, waiting for transfers between devices, on_device(): lax.all_to_all(lax.all_to_all(error_slots, 'dp', split_axis=3, concat_axi...  135 us
    all_gather x1, waiting for transfers between devices, on_device(): lax.all_gather(w_dec, 'dp', axis=1, tiled=True)  80.7 us
    all_to_all x1, blocking collectives, on_device(): lax.all_to_all(error_slots, 'dp', split_axis=3, concat_axis=0, tiled=True)  79.5 us
    all_to_all x1, blocking collectives, on_device(): lax.all_to_all(outgoing, 'latent', split_axis=0, concat_axis=0, tiled=True)  39.9 us
    reshape x2, local copies, waits for them, and re-layouts, on_device(): error_slots = error_slots.reshape(1, owners, capacity, model_width)  30.9 us
    unnamed x6, local copies, waits for them, and re-layouts  27.7 us
    all_to_all x1, local copies, waits for them, and re-layouts, on_device(): lax.all_to_all(error_slots, 'dp', split_axis=3, concat_axis=0, tiled=True)  17.9 us
  transfers between devices with their start and end apart: 4, of which 3 were waited for; matrix products, arithmetic and copies ran while one was open for 2% of the time, Pallas kernels for 0%

commit v1 on v0

v1 whole, which is shorter than its diff:
```python
import jax
import jax.numpy as jnp
from jax import lax
from jax.sharding import PartitionSpec as P

loss_scale = 1.0 / 32.0
MOST = 6


def on_device(activations, owner_ids, block_mask, latent_codes, w_dec, b_dec):
    row_count, visit_count = owner_ids.shape
    block_count = block_mask.shape[2]
    slab_width = latent_codes.shape[2]
    block_width = slab_width // block_count
    model_width = activations.shape[1]
    owners = lax.axis_size("latent")
    groups = lax.axis_size("dp")
    part_width = model_width // groups
    devices = owners * groups
    slots = owners * MOST
    axes = ("dp", "latent")
    bf16 = jnp.bfloat16

    live = block_mask.astype(bf16)[:, :, :, None]
    used = (latent_codes.reshape(row_count, visit_count, block_count, block_width) * live).reshape(
        row_count, visit_count, slab_width
    )
    same = (owner_ids[:, :, None, None] == owner_ids[None, None, :, :]).astype(jnp.float32)
    row = lax.broadcasted_iota(jnp.int32, (row_count, 1, row_count, 1), 0)
    other = lax.broadcasted_iota(jnp.int32, (row_count, 1, row_count, 1), 2)
    position = jnp.sum(jnp.where(other < row, same, 0.0), axis=(2, 3)).astype(jnp.int32)
    target = owner_ids * MOST + position
    placed = (target[:, :, None] == lax.broadcasted_iota(jnp.int32, (1, 1, slots), 2)).astype(bf16)
    outgoing = jnp.einsum("rgs,rgm->sm", placed, used, preferred_element_type=jnp.float32).astype(bf16)
    outgoing = jnp.broadcast_to(
        outgoing.reshape(1, owners, MOST // 2, 2, slab_width), (groups, owners, MOST // 2, 2, slab_width)
    ).reshape(devices, MOST // 2, 2, slab_width)
    arrived = lax.all_to_all(outgoing, axes, split_axis=0, concat_axis=0, tiled=True)
    arrived = arrived.reshape(devices * MOST, slab_width)
    decoded = jnp.dot(arrived, w_dec, preferred_element_type=jnp.float32).astype(bf16)
    returned = lax.all_to_all(
        decoded.reshape(devices, MOST // 2, 2, part_width), axes, split_axis=0, concat_axis=0, tiled=True
    ).reshape(groups, slots, part_width)
    select = placed[:, 0] + placed[:, 1]
    summed = jnp.einsum("rs,dsj->rdj", select, returned, preferred_element_type=jnp.float32)
    rebuilt_wide = b_dec[None, :] + summed.reshape(row_count, model_width)
    errors = (rebuilt_wide - activations.astype(jnp.float32)).astype(bf16)
    error_slots = jnp.einsum(
        "rs,rdj->dsj", select, errors.reshape(row_count, groups, part_width), preferred_element_type=jnp.float32
    ).astype(bf16)
    error_parts = lax.all_to_all(
        error_slots.reshape(devices, MOST // 2, 2, part_width), axes, split_axis=0, concat_axis=0, tiled=True
    ).reshape(devices * MOST, part_width)
    gradient = (
        lax.dot_general(arrived, error_parts, (((0,), (0,)), ((), ())), preferred_element_type=jnp.float32)
        * loss_scale
    )
    return (rebuilt_wide.astype(bf16), gradient.astype(bf16))


def solution(mesh):
    placed = (
        P(("dp", "latent"), None),
        P(("dp", "latent"), None),
        P(("dp", "latent"), None, None),
        P(("dp", "latent"), None, None),
        P("latent", "dp"),
        P(),
    )
    return jax.shard_map(
        on_device,
        mesh=mesh,
        in_specs=placed,
        out_specs=(P(("dp", "latent"), None), P("latent", "dp")),
        check_vma=False,
    )
```

time: 769 us -> 477 us (0.62); the launches traced: 756 us -> 475 us
  waiting for transfers between devices: 398 us -> 140 us
  blocking collectives: 119 us -> 239 us
  local copies, waits for them, and re-layouts: 153 us -> 48.5 us
  other arithmetic: 22.6 us -> 3.98 us
  starting transfers between devices: 23.9 us -> 9.02 us
  between operations: 14.4 us -> 0.71 us
  matrix products: 25.5 us -> 33.5 us
    all_to_all x2 -> x1, waiting for transfers between devices: 317 us -> 140 us  [on_device(): lax.all_to_all(decoded.reshape(devices, MOST // 2, 2, part_width), axes,...]
    all_to_all x2, blocking collectives: 119 us -> 239 us  [the longest x1 149 us: on_device(): lax.all_to_all(error_slots.reshape(devices, MOST // 2, 2, part_width), ax...]
    all_gather x2 -> x0, waiting for transfers between devices: 80.7 us -> none  [the longest x1 80.7 us: on_device(): lax.all_gather(w_dec, 'dp', axis=1, tiled=True)]
    all_to_all x3 -> x0, local copies, waits for them, and re-layouts: 28.2 us -> none  [the longest x1 17.9 us: on_device(): lax.all_to_all(error_slots, 'dp', split_axis=3, concat_axis=0, tiled=True)]
    unnamed x6 -> x2, local copies, waits for them, and re-layouts: 27.7 us -> 0.01 us
    reshape x9 -> x5, local copies, waits for them, and re-layouts: 58.2 us -> 38.3 us  [the longest x1 10.9 us: on_device(): decoded.reshape(devices, MOST // 2, 2, part_width)]
    all_to_all x2 -> x1, starting transfers between devices: 23.5 us -> 9.02 us  [on_device(): lax.all_to_all(decoded.reshape(devices, MOST // 2, 2, part_width), axes,...]
    reduce_sum x3 -> x1, other arithmetic: 15 us -> 0.93 us  [on_device(): jnp.sum(jnp.where(other < row, same, 0.0), axis=(2, 3)).astype(jnp.int32)]
  transfers between devices with their start and end apart: 4 -> 1, of which waited for: 3 -> 1; matrix products, arithmetic and copies ran while one was open for 2% -> 0% of each run, Pallas kernels for 0% -> 0%
where the time goes in v1:
time: 477 us; the launch traced here: 475 us
  blocking collectives  239 us (50%)
  waiting for transfers between devices  140 us (29%)
  local copies, waits for them, and re-layouts  48.5 us (10%)
  matrix products  33.5 us (7%)
  starting transfers between devices  9.02 us (2%)
    all_to_all x1, blocking collectives, on_device(): lax.all_to_all(error_slots.reshape(devices, MOST // 2, 2, part_width), ax...  149 us
    all_to_all x1, waiting for transfers between devices, on_device(): lax.all_to_all(decoded.reshape(devices, MOST // 2, 2, part_width), axes,...  140 us
    all_to_all x1, blocking collectives, on_device(): lax.all_to_all(outgoing, axes, split_axis=0, concat_axis=0, tiled=True)  90.1 us
    dot_general x1, matrix products, on_device(): jnp.dot(arrived, w_dec, preferred_element_type=jnp.float32).astype(bf16)  11.2 us
    reshape x1, local copies, waits for them, and re-layouts, on_device(): decoded.reshape(devices, MOST // 2, 2, part_width)  10.9 us
    reshape x1, local copies, waits for them, and re-layouts, on_device(): error_slots.reshape(devices, MOST // 2, 2, part_width)  10.9 us
    dot_general x1, matrix products, on_device(): lax.dot_general(arrived, error_parts, (((0,), (0,)), ((), ())), preferred...  10.6 us
    reshape x1, local copies, waits for them, and re-layouts, on_device(): returned = lax.all_to_all(decoded.reshape(devices, MOST // 2, 2, part_wid...  10.2 us
  transfers between devices with their start and end apart: 1, of which 1 were waited for; matrix products, arithmetic and copies ran while one was open for 0% of the time, Pallas kernels for 0%

profile of v1, /device:TPU:1, one launch (start us, length us, event | category | flops | bytes accessed | tf_op | source)
XLA Modules:
  0.0 474.9 jit_solution(18271228753102382734)
XLA Ops:
  0.7 0.7 convert_element_type.39
  1.4 0.9 select_reduce_fusion
  2.3 0.7 convert_add_fusion
  3.0 0.1 copy.44
  3.1 0.3 mul.25
  3.4 0.1 mul.26
  3.6 1.6 mul.27
  5.2 0.4 bitcast_convert_fusion
  5.6 0.3 broadcast_in_dim.26
  5.9 0.2 copy.46
  6.1 0.4 broadcast_in_dim.27
  6.5 3.2 copy.47
  9.7 90.1 %all_to_all.15 = bf16[256,3,2,1024]{3,2,1,0:T(2,128)(2,1)S(1)} all-to-all(bf16[256,3,2,1024]{3,2,1,0:T(2,128)(2,1)S(1)} %copy.47), channel_id=1, replica_groups=mesh['dp'=4,'latent'=64] {'dp','latent'}, dimensions={0} | all-to-all | bytes 6291456 | tf_op jit(solution)/shard_map/all_to_all | solution.py:38
  99.8 3.2 reshape.46
  103.0 11.2 %convolution_convert_fusion = bf16[1536,2048]{1,0:T(8,128)(2,1)} fusion(bf16[1536,1024]{1,0:T(8,128)(2,1)} %reshape.46, bf16[1024,2048]{1,0:T(8,128)(2,1)} %param.10), kind=kOutput, calls=%fused_computation.3 | convolution fusion | flops 6445596672 | bytes 13631488 | tf_op jit(solution)/shard_map/dot_general | solution.py:40
  114.2 10.9 %reshape.47 = bf16[256,3,2,2048]{3,2,1,0:T(2,128)(2,1)} reshape(bf16[1536,2048]{1,0:T(8,128)(2,1)} %convolution_convert_fusion) | data formatting | bytes 12582912 | tf_op jit(solution)/shard_map/reshape | solution.py:42
  125.1 9.0 %all-to-all-start.1 = ((bf16[256,3,2,2048]{3,2,1,0:T(2,128)(2,1)}), bf16[256,3,2,2048]{3,2,1,0:T(2,128)(2,1)}, u32[]{:S(2)}, u32[]{:S(2)}) async-start(bf16[256,3,2,2048]{3,2,1,0:T(2,128)(2,1)} %reshape.47), calls=%async_computation.1 | async-start | bytes 12582912 | tf_op jit(solution)/shard_map/all_to_all | solution.py:41
  134.1 0.1 fusion.9
  134.2 140.1 %all-to-all-done.1 = bf16[256,3,2,2048]{3,2,1,0:T(2,128)(2,1)} async-done(((bf16[256,3,2,2048]{3,2,1,0:T(2,128)(2,1)}), bf16[256,3,2,2048]{3,2,1,0:T(2,128)(2,1)}, u32[]{:S(2)}, u32[]{:S(2)}) %all-to-all-start.1) | async-done | bytes 6291488 | tf_op jit(solution)/shard_map/all_to_all | solution.py:41
  274.3 10.2 %reshape.48 = bf16[4,384,2048]{2,1,0:T(8,128)(2,1)} reshape(bf16[256,3,2,2048]{3,2,1,0:T(2,128)(2,1)} %all-to-all-done.1) | data formatting | bytes 12582912 | tf_op jit(solution)/shard_map/reshape | solution.py:43
  284.5 0.0 copy-start
  284.5 8.7 %copy.48 = bf16[4,2048,384]{2,1,0:T(8,128)(2,1)} copy(bf16[4,2048,384]{1,2,0:T(8,128)(2,1)} %bitcast.31) | data formatting | bytes 12582912 | tf_op jit(solution)/shard_map/rs,dsj->rdj/dot_general | solution.py:45
  293.1 0.0 copy-done
  293.1 6.9 %subtract_convert_fusion = (bf16[128,8192]{1,0:T(8,128)(2,1)S(1)}, bf16[128,8192]{1,0:T(8,128)(2,1)}) fusion(bf16[128,8192]{1,0:T(8,128)(2,1)} %param.6, bf16[8192,384]{1,0:T(8,128)(2,1)} %bitcast.30, bf16[128,2,384]{0,2,1:T(8,128)(2,1)S(1)} %fusion.9, f32[8192]{0:T(1024)S(1)} %copy-done), kind=kOutput, calls=%fused_computation.7 | convolution fusion | flops 810598400 | bytes 12812288 | tf_op jit(solution)/shard_map/rs,dsj->rdj/dot_general | solution.py:45
  300.0 4.4 convert_bitcast_fusion
  304.4 10.9 %reshape.50 = bf16[256,3,2,2048]{3,2,1,0:T(2,128)(2,1)} reshape(bf16[4,384,2048]{2,1,0:T(8,128)(2,1)} %convert_bitcast_fusion) | data formatting | bytes 12582912 | tf_op jit(solution)/shard_map/reshape | solution.py:52
  315.3 149.0 %all_to_all.16 = bf16[256,3,2,2048]{3,2,1,0:T(2,128)(2,1)S(1)} all-to-all(bf16[256,3,2,2048]{3,2,1,0:T(2,128)(2,1)} %reshape.50), channel_id=1, replica_groups=mesh['dp'=4,'latent'=64] {'dp','latent'}, dimensions={0} | all-to-all | bytes 12582912 | tf_op jit(solution)/shard_map/all_to_all | solution.py:51
  464.3 10.6 %fusion = bf16[1024,2048]{1,0:T(8,128)(2,1)} fusion(bf16[256,3,2,2048]{3,2,1,0:T(2,128)(2,1)S(1)} %all_to_all.16, bf16[256,3,2,1024]{3,2,1,0:T(2,128)(2,1)S(1)} %all_to_all.15), kind=kOutput, calls=%fused_computation.2 | convolution fusion | flops 6446645248 | bytes 13631488 | tf_op jit(solution)/shard_map/dot_general | solution.py:55
  (1 shorter events, 0.0 us)
Async XLA Ops:
  125.1 149.2 %all-to-all-start.1 = ((bf16[256,3,2,2048]{3,2,1,0:T(2,128)(2,1)}), bf16[256,3,2,2048]{3,2,1,0:T(2,128)(2,1)}, u32[]{:S(2)}, u32[]{:S(2)}) async-start(bf16[256,3,2,2048]{3,2,1,0:T(2,128)(2,1)} %reshape.47), calls=%async_computation.1 | async-start | bytes 12582912 | tf_op jit(solution)/shard_map/all_to_all | solution.py:41
  284.5 8.7 %copy-start = (f32[8192]{0:T(1024)S(1)}, f32[8192]{0:T(1024)}, u32[]{:S(2)}) copy-start(f32[8192]{0:T(1024)} %param.11) | copy-start | bytes 98308

commit v2 on v1

--- a/solution.py
+++ b/solution.py
@@ -1,10 +1,50 @@
 import jax
 import jax.numpy as jnp
 from jax import lax
+from jax.experimental import pallas as pl
+from jax.experimental.pallas import tpu as pltpu
 from jax.sharding import PartitionSpec as P
 
 loss_scale = 1.0 / 32.0
 MOST = 6
+
+
+def exchange_kernel(x_ref, o_ref, send_sem, recv_sem, own_sem):
+    dp = lax.axis_index("dp")
+    latent = lax.axis_index("latent")
+    own = pltpu.make_async_copy(x_ref.at[dp * 64 + latent], o_ref.at[dp * 64 + latent], own_sem)
+    own.start()
+
+    def step(k, carry):
+        ko = k % 64
+        to_dp = (dp + k // 64) % 4
+        to_latent = ((latent // 16 + ko // 16) % 4) * 16 + ((latent // 8 + ko // 8) % 2) * 8 + (latent + ko) % 8
+        pltpu.make_async_remote_copy(
+            x_ref.at[to_dp * 64 + to_latent],
+            o_ref.at[dp * 64 + latent],
+            send_sem,
+            recv_sem,
+            device_id=(to_dp, to_latent),
+            device_id_type=pl.DeviceIdType.MESH,
+        ).start()
+        return carry
+
+    lax.fori_loop(1, 256, step, 0)
+    own.wait()
+    rest = o_ref.at[pl.ds(0, 255)]
+    pltpu.make_async_copy(rest, rest, send_sem).wait()
+    pltpu.make_async_copy(rest, rest, recv_sem).wait()
+
+
+def exchange(x):
+    return pl.pallas_call(
+        exchange_kernel,
+        out_shape=jax.ShapeDtypeStruct(x.shape, x.dtype),
+        in_specs=[pl.BlockSpec(memory_space=pl.ANY)],
+        out_specs=pl.BlockSpec(memory_space=pl.ANY),
+        scratch_shapes=[pltpu.SemaphoreType.DMA] * 3,
+        compiler_params=pltpu.CompilerParams(has_side_effects=True),
+    )(x)
 
 
 def on_device(activations, owner_ids, block_mask, latent_codes, w_dec, b_dec):
@@ -32,15 +72,13 @@
     target = owner_ids * MOST + position
     placed = (target[:, :, None] == lax.broadcasted_iota(jnp.int32, (1, 1, slots), 2)).astype(bf16)
     outgoing = jnp.einsum("rgs,rgm->sm", placed, used, preferred_element_type=jnp.float32).astype(bf16)
-    outgoing = jnp.broadcast_to(
-        outgoing.reshape(1, owners, MOST // 2, 2, slab_width), (groups, owners, MOST // 2, 2, slab_width)
-    ).reshape(devices, MOST // 2, 2, slab_width)
-    arrived = lax.all_to_all(outgoing, axes, split_axis=0, concat_axis=0, tiled=True)
+    arrived = lax.all_to_all(
+        outgoing.reshape(owners, MOST // 2, 2, slab_width), "latent", split_axis=0, concat_axis=0, tiled=True
+    )
+    arrived = lax.all_gather(arrived, "dp", axis=0, tiled=True)
     arrived = arrived.reshape(devices * MOST, slab_width)
     decoded = jnp.dot(arrived, w_dec, preferred_element_type=jnp.float32).astype(bf16)
-    returned = lax.all_to_all(
-        decoded.reshape(devices, MOST // 2, 2, part_width), axes, split_axis=0, concat_axis=0, tiled=True
-    ).reshape(groups, slots, part_width)
+    returned = exchange(decoded.reshape(devices, MOST // 2, 2, part_width)).reshape(groups, slots, part_width)
     select = placed[:, 0] + placed[:, 1]
     summed = jnp.einsum("rs,dsj->rdj", select, returned, preferred_element_type=jnp.float32)
     rebuilt_wide = b_dec[None, :] + summed.reshape(row_count, model_width)

time: 477 us -> 473 us (level)
  Pallas kernels: 0 us -> 155 us
  waiting for transfers between devices: 140 us -> 34.7 us
  blocking collectives: 239 us -> 181 us
  between operations: 0.71 us -> 14.1 us
  starting transfers between devices: 9.02 us -> 0.04 us
    pallas_call x0 -> x1, Pallas kernels: none -> 155 us  [exchange(): pl.pallas_call(exchange_kernel, out_shape=jax.ShapeDtypeStruct(x.shape, x...]
    all_to_all x1 -> x0, waiting for transfers between devices: 140 us -> none  [on_device(): lax.all_to_all(decoded.reshape(devices, MOST // 2, 2, part_width), axes,...]
    all_to_all x1, blocking collectives: 90.1 us -> 34.6 us  [on_device(): lax.all_to_all(outgoing.reshape(owners, MOST // 2, 2, slab_width), 'laten...]
    all_gather x0 -> x1, waiting for transfers between devices: none -> 34.7 us  [on_device(): arrived = lax.all_gather(arrived, 'dp', axis=0, tiled=True)]
    all_to_all x1 -> x0, starting transfers between devices: 9.02 us -> none  [on_device(): lax.all_to_all(decoded.reshape(devices, MOST // 2, 2, part_width), axes,...]
    dot_general x1 -> x0, local copies, waits for them, and re-layouts: 8.66 us -> none  [on_device(): jnp.einsum('rs,dsj->rdj', select, returned, preferred_element_type=jnp.fl...]
    reshape x2 -> x3, local copies, waits for them, and re-layouts: 13.4 us -> 19.2 us  [the longest x2 18.9 us: on_device(): exchange(decoded.reshape(devices, MOST // 2, 2, part_width))]
    all_gather x0 -> x1, local copies, waits for them, and re-layouts: none -> 5.12 us  [on_device(): arrived = lax.all_gather(arrived, 'dp', axis=0, tiled=True)]
where the time goes in v2:
time: 473 us; the launch traced here: 471 us
  blocking collectives  181 us (38%)
  Pallas kernels  155 us (33%)
  local copies, waits for them, and re-layouts  51 us (11%)
  waiting for transfers between devices  34.7 us (7%)
  matrix products  31.8 us (7%)
  between operations  14.1 us (3%)
    pallas_call x1, Pallas kernels, exchange(): pl.pallas_call(exchange_kernel, out_shape=jax.ShapeDtypeStruct(x.shape, x...  155 us
    all_to_all x1, blocking collectives, on_device(): lax.all_to_all(error_slots.reshape(devices, MOST // 2, 2, part_width), ax...  147 us
    all_gather x1, waiting for transfers between devices, on_device(): arrived = lax.all_gather(arrived, 'dp', axis=0, tiled=True)  34.7 us
    all_to_all x1, blocking collectives, on_device(): lax.all_to_all(outgoing.reshape(owners, MOST // 2, 2, slab_width), 'laten...  34.6 us
    reshape x2, local copies, waits for them, and re-layouts, on_device(): exchange(decoded.reshape(devices, MOST // 2, 2, part_width))  18.9 us
    dot_general x1, matrix products, on_device(): jnp.dot(arrived, w_dec, preferred_element_type=jnp.float32).astype(bf16)  11.1 us
    reshape x1, local copies, waits for them, and re-layouts, on_device(): error_slots.reshape(devices, MOST // 2, 2, part_width)  10.9 us
    reshape x1, local copies, waits for them, and re-layouts, on_device(): decoded.reshape(devices, MOST // 2, 2, part_width)  10.9 us
  transfers between devices with their start and end apart: 1, of which 1 were waited for; matrix products, arithmetic and copies ran while one was open for 0% of the time, Pallas kernels for 0%

profile of v2, /device:TPU:1, one launch (start us, length us, event | category | flops | bytes accessed | tf_op | source)
XLA Modules:
  0.0 471.3 jit_solution(17374731921214518377)
XLA Ops:
  7.2 0.0 all-gather.2.cloned.1.call-start
  7.2 0.7 convert_element_type.39
  7.9 0.9 select_reduce_fusion
  8.9 0.7 convert_add_fusion
  9.6 0.1 copy.33
  9.7 0.3 mul.25
  10.0 0.1 mul.26
  10.2 1.6 mul.27
  11.7 0.4 bitcast_convert_fusion
  12.1 0.3 reshape.43
  12.5 34.6 %all_to_all.10 = bf16[64,3,2,1024]{3,2,1,0:T(2,128)(2,1)S(1)} all-to-all(bf16[64,3,2,1024]{3,2,1,0:T(2,128)(2,1)S(1)} %reshape.43), channel_id=1, replica_groups=mesh['dp'=4,'latent'=64] {'latent'}, dimensions={0} | all-to-all | bytes 1572864 | tf_op jit(solution)/shard_map/all_to_all | solution.py:75
  47.0 1.1 copy.35
  48.1 0.0 all-gather.2.cloned.1.call-update
  48.1 0.1 fusion.8
  48.2 34.7 %all-gather.2.cloned.1.call-done = bf16[256,3,2,1024]{3,0,2,1:T(8,128)(2,1)} async-done(((bf16[64,3,2,1024]{3,0,2,1:T(8,128)(2,1)}), bf16[256,3,2,1024]{3,0,2,1:T(8,128)(2,1)}) %all-gather.2.cloned.1.call-update) | async-done | bytes 3145744 | tf_op jit(solution)/shard_map/all_gather | solution.py:78
  82.9 5.1 %copy.36 = bf16[256,3,2,1024]{3,2,1,0:T(2,128)(2,1)S(1)} copy(bf16[256,3,2,1024]{3,0,2,1:T(8,128)(2,1)} %all-gather.2.cloned.1.call-done) | data formatting | bytes 6291456 | tf_op jit(solution)/shard_map/all_gather | solution.py:78
  88.0 3.2 reshape.44
  91.2 11.1 %convolution_convert_fusion = bf16[1536,2048]{1,0:T(8,128)(2,1)} fusion(bf16[1536,1024]{1,0:T(8,128)(2,1)} %reshape.44, bf16[1024,2048]{1,0:T(8,128)(2,1)} %param.10), kind=kOutput, calls=%fused_computation.3 | convolution fusion | flops 6445596672 | bytes 13631488 | tf_op jit(solution)/shard_map/dot_general | solution.py:80
  102.3 10.9 %reshape.45.x_ref = bf16[256,3,2,2048]{3,2,1,0:T(2,128)(2,1)} reshape(bf16[1536,2048]{1,0:T(8,128)(2,1)} %convolution_convert_fusion) | data formatting | bytes 12582912 | tf_op jit(solution)/shard_map/reshape | solution.py:81
  113.2 154.5 %shard_map.77 = bf16[256,3,2,2048]{3,2,1,0:T(2,128)(2,1)} custom-call(bf16[256,3,2,2048]{3,2,1,0:T(2,128)(2,1)} %reshape.45.x_ref), custom_call_target="tpu_custom_call" | custom-call | tf_op jit(solution)/shard_map/pallas_call | solution.py:40
  267.7 10.1 %reshape.46 = bf16[4,384,2048]{2,1,0:T(8,128)(2,1)} reshape(bf16[256,3,2,2048]{3,2,1,0:T(2,128)(2,1)} %shard_map.77) | data formatting | bytes 12582912 | tf_op jit(solution)/shard_map/reshape | solution.py:81
  277.9 0.0 copy-start.1
  277.9 0.0 copy-start.2
  277.9 8.8 %copy.37 = bf16[4,384,2048]{1,2,0:T(8,128)(2,1)} copy(bf16[4,384,2048]{2,1,0:T(8,128)(2,1)} %reshape.46) | data formatting | bytes 12582912 | tf_op jit(solution)/shard_map/reshape | solution.py:81
  286.6 0.0 copy-done.1
  286.6 0.0 copy-done.2
  286.6 6.3 %subtract_convert_fusion = (bf16[128,8192]{1,0:T(8,128)(2,1)S(1)}, bf16[128,8192]{1,0:T(8,128)(2,1)}) fusion(bf16[128,8192]{1,0:T(8,128)(2,1)S(1)} %copy-done.1, bf16[8192,384]{1,0:T(8,128)(2,1)} %bitcast.31, bf16[128,2,384]{0,2,1:T(8,128)(2,1)S(1)} %fusion.8, f32[8192]{0:T(1024)S(1)} %copy-done.2), kind=kOutput, calls=%fused_computation.7 | convolution fusion | flops 810598400 | bytes 12812288 | tf_op jit(solution)/shard_map/rs,dsj->rdj/dot_general | solution.py:83
  292.9 4.4 convert_bitcast_fusion
  297.3 10.9 %reshape.48 = bf16[256,3,2,2048]{3,2,1,0:T(2,128)(2,1)} reshape(bf16[4,384,2048]{2,1,0:T(8,128)(2,1)} %convert_bitcast_fusion) | data formatting | bytes 12582912 | tf_op jit(solution)/shard_map/reshape | solution.py:90
  308.2 146.7 %all_to_all.11 = bf16[256,3,2,2048]{3,2,1,0:T(2,128)(2,1)S(1)} all-to-all(bf16[256,3,2,2048]{3,2,1,0:T(2,128)(2,1)} %reshape.48), channel_id=1, replica_groups=mesh['dp'=4,'latent'=64] {'dp','latent'}, dimensions={0} | all-to-all | bytes 12582912 | tf_op jit(solution)/shard_map/all_to_all | solution.py:89
  454.9 0.0 copy-done
  454.9 9.6 %fusion = bf16[1024,2048]{1,0:T(8,128)(2,1)} fusion(bf16[256,3,2,1024]{3,0,2,1:T(8,128)(2,1)S(1)} %copy-done, bf16[256,3,2,2048]{3,2,1,0:T(2,128)(2,1)S(1)} %all_to_all.11), kind=kOutput, calls=%fused_computation.2 | convolution fusion | flops 6446645248 | bytes 13631488 | tf_op jit(solution)/shard_map/dot_general | solution.py:93
  (2 shorter events, 0.0 us)
Async XLA Ops:
  7.2 75.7 %all-gather.2.cloned.1.call-start = ((), (), s32[]{:S(2)}) async-start(), calls=%async_computation.2 | async-start | bytes 3932160 | tf_op jit(solution)/shard_map/all_gather | solution.py:78
  277.9 8.8 %copy-start.1 = (bf16[128,8192]{1,0:T(8,128)(2,1)S(1)}, bf16[128,8192]{1,0:T(8,128)(2,1)}, u32[]{:S(2)}) copy-start(bf16[128,8192]{1,0:T(8,128)(2,1)} %param.6) | copy-start | bytes 6291460
  277.9 8.8 %copy-start.2 = (f32[8192]{0:T(1024)S(1)}, f32[8192]{0:T(1024)}, u32[]{:S(2)}) copy-start(f32[8192]{0:T(1024)} %param.11) | copy-start | bytes 98308
  308.2 146.7 %copy-start = (bf16[256,3,2,1024]{3,0,2,1:T(8,128)(2,1)S(1)}, bf16[256,3,2,1024]{3,0,2,1:T(8,128)(2,1)}, u32[]{:S(2)}) copy-start(bf16[256,3,2,1024]{3,0,2,1:T(8,128)(2,1)} %all-gather.2.cloned.1.call-done) | copy-start | bytes 9437188
Sparse Core Ops, SparseCore 0:
  48.3 34.5 all-gather.1

commit v3 on v1

v3 whole, which is shorter than its diff:
```python
import jax
import jax.numpy as jnp
import numpy as np
from jax import lax
from jax.experimental import pallas as pl
from jax.experimental.pallas import tpu as pltpu
from jax.sharding import PartitionSpec as P

loss_scale = 1.0 / 32.0
MOST = 6
PAD = 8
PEERS = 8
PARTS = 8
GROUPS = 4
OWNERS = 64
HALF = OWNERS // 2
RUNS = OWNERS // PEERS
BATCH = PEERS * PAD
STACK = PARTS * BATCH
SENT = PARTS * MOST
BF16, F32 = jnp.bfloat16, jnp.float32
MESH = pl.DeviceIdType.MESH


def message_order():
    out = np.zeros((PARTS, PEERS, PAD, PEERS, PARTS, MOST), np.float32)
    for part in range(PARTS):
        for peer in range(PEERS):
            for slot in range(MOST):
                out[part, peer, slot, peer, part, slot] = 1
    return out.reshape(STACK, PEERS * SENT)


def dot(a, b):
    return jnp.dot(a, b, preferred_element_type=F32)


def shifted(latent, offset, sign):
    y = (latent // 16 + sign * (offset // 16) + 4) % 4
    x = (latent // 8 + offset // 8) % 2
    z = (latent % 8 + sign * (offset % 8) + 8) % 8
    return y * 16 + x * 8 + z


def bytes_wait(ref, sem):
    pltpu.make_async_copy(ref, ref, sem).wait()


def kernel(
    rel_ref, mask_ref, codes_ref, bias_ref, spread_ref, pack_ref, act_hbm, w_hbm,
    rebuilt_hbm, grad_hbm,
    w_ref, act_ref, rebuilt_ref, take_ref, put_ref, codes_out, codes_in, codes_t, codes_rows,
    code_tmp, term_tmp, sent, terms_in, errors_in, wide_tmp, error_tmp, error_rows, total, stage,
    load_sem, own_sem, code_send, code_recv, copy_send, copy_recv, term_send, term_recv,
    error_send, error_recv, rebuilt_sem, stage_sem,
):
    dp = lax.axis_index("dp")
    latent = lax.axis_index("latent")
    rows = act_ref.shape[0]
    load_w = pltpu.make_async_copy(w_hbm, w_ref, load_sem.at[0])
    load_act = pltpu.make_async_copy(act_hbm, act_ref, load_sem.at[1])
    load_w.start()
    load_act.start()

    down = lax.broadcasted_iota(jnp.int32, (rows, rows), 0)
    across = lax.broadcasted_iota(jnp.int32, (rows, rows), 1)
    along = [jnp.broadcast_to(rel_ref[g : g + 1, :], (rows, rows)) for g in range(2)]
    below = [jnp.transpose(a) for a in along]
    slot_lane = lax.broadcasted_iota(jnp.int32, (rows, OWNERS * PAD), 1).astype(F32)
    slot_row = lax.broadcasted_iota(jnp.int32, (OWNERS * PAD, rows), 0).astype(F32)
    take = jnp.zeros((rows, OWNERS * PAD), F32)
    puts = []
    for g in range(2):
        count = [jnp.where(below[g] == along[o], 1.0, 0.0) for o in range(2)]
        here = below[g][:, :1] + jnp.sum(jnp.where(across < down, count[0] + count[1], 0.0), axis=1, keepdims=True)
        take = take + jnp.where(slot_lane == here, 1.0, 0.0)
        count = [jnp.where(below[o] == along[g], 1.0, 0.0) for o in range(2)]
        here = rel_ref[g : g + 1, :] + jnp.sum(jnp.where(down < across, count[0] + count[1], 0.0), axis=0, keepdims=True)
        puts.append(jnp.where(slot_row == here, 1.0, 0.0))
    take_ref[...] = take.astype(BF16)
    put_ref[...] = (puts[0] + puts[1]).astype(BF16)
    width = codes_ref.shape[1] // 2
    block = width // PARTS
    for part in range(PARTS):
        placed = jnp.zeros((OWNERS * PAD, block), F32)
        for g in range(2):
            live = mask_ref[g, part : part + 1, :].astype(F32)
            start = g * width + part * block
            placed = placed + dot((puts[g] * live).astype(BF16), codes_ref[:, start : start + block])
        code_tmp[:, part] = placed.astype(BF16).reshape(RUNS, BATCH, block)

    def send_codes(run, carry):
        message = dot(pack_ref[...], code_tmp[run].reshape(STACK, block)).astype(BF16)
        codes_out[pl.ds(run * PEERS, PEERS)] = message.reshape(PEERS, SENT, block)

        def one(i, c):
            ko = run * PEERS + i
            pltpu.make_async_remote_copy(
                codes_out.at[ko], codes_in.at[0, ko], code_send, code_recv.at[run // (RUNS // 2)],
                device_id=(dp, shifted(latent, ko, 1)), device_id_type=MESH,
            ).start()
            return c

        lax.fori_loop(jnp.where(run == 0, 1, 0), PEERS, one, 0)
        return carry

    lax.fori_loop(0, RUNS, send_codes, 0)
    own = pltpu.make_async_copy(codes_out.at[0], codes_in.at[0, 0], own_sem.at[0])
    own.start()
    own.wait()
    unit = lax.broadcasted_iota(jnp.int32, (block, block), 0) == lax.broadcasted_iota(jnp.int32, (block, block), 1)
    unit = jnp.where(unit, 1.0, 0.0).astype(BF16)
    columns = w_ref.shape[1] // PARTS

    def forward(kd, half):
        def spread(g, carry):
            got = codes_in[kd, pl.ds(half * HALF + g * PEERS, PEERS)].reshape(PEERS * SENT, block)
            flat = dot(spread_ref[...], got).astype(BF16)
            for part in range(PARTS):
                codes_rows[pl.ds(g * BATCH, BATCH), part * block : (part + 1) * block] = flat[
                    part * BATCH : (part + 1) * BATCH
                ]
            return carry

        lax.fori_loop(0, RUNS // 2, spread, 0)

        def decode(n, carry):
            at = pl.ds(pl.multiple_of(n * columns, columns), columns)
            term = dot(codes_rows[...], w_ref[:, at]).astype(BF16)
            term_tmp[:, n] = term.reshape(RUNS // 2, BATCH, columns)
            return carry

        lax.fori_loop(0, PARTS, decode, 0)

        def pack(g, carry):
            run = half * (RUNS // 2) + g
            message = dot(pack_ref[...], term_tmp[g].reshape(STACK, columns)).astype(BF16)
            sent[kd, pl.ds(run * PEERS, PEERS)] = message.reshape(PEERS, SENT, columns)

            def one(i, c):
                ko = run * PEERS + i
                pltpu.make_async_remote_copy(
                    sent.at[kd, ko], terms_in.at[kd, ko], term_send.at[kd], term_recv.at[kd],
                    device_id=((dp - kd + GROUPS) % GROUPS, shifted(latent, ko, -1)), device_id_type=MESH,
                ).start()
                return c

            lax.fori_loop(jnp.where(run == 0, 1, 0) if kd == 0 else 0, PEERS, one, 0)
            return carry

        lax.fori_loop(0, RUNS // 2, pack, 0)
        for part in range(PARTS):
            turned = lax.dot_general(
                unit, codes_rows[:, part * block : (part + 1) * block], (((1,), (1,)), ((), ())),
                preferred_element_type=F32,
            )
            codes_t[kd, part * block : (part + 1) * block, half * HALF * PAD : (half + 1) * HALF * PAD] = turned.astype(BF16)

    copies = []
    for half in range(2):
        first = 1 if half == 0 else HALF
        bytes_wait(codes_in.at[0, first : (half + 1) * HALF], code_recv.at[half])
        for kd in range(1, GROUPS):
            copy = pltpu.make_async_remote_copy(
                codes_in.at[0, pl.ds(half * HALF, HALF)], codes_in.at[kd, pl.ds(half * HALF, HALF)],
                copy_send.at[half, kd - 1], copy_recv.at[half, kd - 1],
                device_id=((dp + kd) % GROUPS, latent), device_id_type=MESH,
            )
            copy.start()
            copies.append((kd, half, copy))
        if half == 0:
            load_w.wait()
        forward(0, half)
    own_term = pltpu.make_async_copy(sent.at[0, 0], terms_in.at[0, 0], own_sem.at[1])
    own_term.start()
    for kd in range(1, GROUPS):
        for half in range(2):
            for ckd, chalf, copy in copies:
                if ckd == kd and chalf == half:
                    copy.wait_recv()
            forward(kd, half)
    own_term.wait()
    load_act.wait()

    stores = []
    for kd in range(GROUPS):
        first = 1 if kd == 0 else 0
        bytes_wait(terms_in.at[kd, first:OWNERS], term_recv.at[kd])

        def spread(run, carry):
            got = terms_in[kd, pl.ds(run * PEERS, PEERS)].reshape(PEERS * SENT, columns)
            flat = dot(spread_ref[...], got).astype(BF16)
            wide_tmp[:, pl.ds(run * BATCH, BATCH), :] = flat.reshape(PARTS, BATCH, columns)
            return carry

        lax.fori_loop(0, RUNS, spread, 0)
        slab = (dp + kd) % GROUPS

        def combine(part, carry):
            at = pl.ds(pl.multiple_of((slab * PARTS + part) * columns, columns), columns)
            wide = dot(take_ref[...], wide_tmp[part]) + bias_ref[:, at]
            rebuilt_ref[:, at] = wide.astype(BF16)
            error = (wide - act_ref[:, at].astype(F32)).astype(BF16)
            error_tmp[:, part] = dot(put_ref[...], error).astype(BF16).reshape(RUNS, BATCH, columns)
            return carry

        lax.fori_loop(0, PARTS, combine, 0)
        at = pl.ds(pl.multiple_of(slab * PARTS * columns, PARTS * columns), PARTS * columns)
        store = pltpu.make_async_copy(rebuilt_ref.at[:, at], rebuilt_hbm.at[:, at], rebuilt_sem.at[kd])
        store.start()
        stores.append(store)
        bytes_wait(sent.at[kd, first:OWNERS], term_send.at[kd])

        def pack(run, carry):
            message = dot(pack_ref[...], error_tmp[run].reshape(STACK, columns)).astype(BF16)
            sent[kd, pl.ds(run * PEERS, PEERS)] = message.reshape(PEERS, SENT, columns)

            def one(i, c):
                ko = run * PEERS + i
                pltpu.make_async_remote_copy(
                    sent.at[kd, ko], errors_in.at[kd, ko], error_send.at[kd], error_recv.at[kd],
                    device_id=((dp + kd) % GROUPS, shifted(latent, ko, 1)), device_id_type=MESH,
                ).start()
                return c

            lax.fori_loop(jnp.where(run == 0, 1, 0) if kd == 0 else 0, PEERS, one, 0)
            return carry

        lax.fori_loop(0, RUNS, pack, 0)
        if kd == 0:
            own_error = pltpu.make_async_copy(sent.at[0, 0], errors_in.at[0, 0], own_sem.at[2])
            own_error.start()
    own_error.wait()

    for kd in range(GROUPS):
        first = 1 if kd == 0 else 0
        bytes_wait(errors_in.at[kd, first:OWNERS], error_recv.at[kd])

        def spread(run, carry):
            got = errors_in[kd, pl.ds(run * PEERS, PEERS)].reshape(PEERS * SENT, columns)
            flat = dot(spread_ref[...], got).astype(BF16)
            for part in range(PARTS):
                error_rows[pl.ds(run * BATCH, BATCH), part * columns : (part + 1) * columns] = flat[
                    part * BATCH : (part + 1) * BATCH
                ]
            return carry

        lax.fori_loop(0, RUNS, spread, 0)
        if kd < GROUPS - 1:

            def accumulate(n, carry):
                at = pl.ds(pl.multiple_of(n * columns, columns), columns)
                more = dot(codes_t[kd], error_rows[:, at])
                total[:, at] = more if kd == 0 else total[:, at] + more
                return carry

            lax.fori_loop(0, PARTS, accumulate, 0)
        else:
            writes = []
            for n in range(PARTS):
                at = slice(n * columns, (n + 1) * columns)
                more = dot(codes_t[kd], error_rows[:, at])
                slot = n % stage.shape[0]
                if n >= stage.shape[0]:
                    writes[n - stage.shape[0]].wait()
                stage[slot] = ((total[:, at] + more) * loss_scale).astype(BF16)
                write = pltpu.make_async_copy(stage.at[slot], grad_hbm.at[:, at], stage_sem.at[slot])
                write.start()
                writes.append(write)
            for write in writes[-stage.shape[0] :]:
                write.wait()
    for store in stores:
        store.wait()
    bytes_wait(codes_out.at[1:OWNERS], code_send)
    for _, _, copy in copies:
        copy.wait_send()
    for kd in range(GROUPS):
        bytes_wait(sent.at[kd, (1 if kd == 0 else 0) : OWNERS], error_send.at[kd])


def on_device(activations, owner_ids, block_mask, latent_codes, w_dec, b_dec):
    rows, model_width = activations.shape
    slab, part_width = w_dec.shape
    block, columns = slab // PARTS, part_width // PARTS
    latent = lax.axis_index("latent")
    owner = owner_ids.T
    relative = (
        (owner // 16 - latent // 16) % 4 * 16 + (owner // 8 - latent // 8) % 2 * 8 + (owner - latent) % 8
    )
    order = message_order()
    vmem = pl.BlockSpec(memory_space=pltpu.VMEM)
    hbm = pl.BlockSpec(memory_space=pl.ANY)
    dma = pltpu.SemaphoreType.DMA
    return pl.pallas_call(
        kernel,
        out_shape=(
            jax.ShapeDtypeStruct((rows, model_width), BF16),
            jax.ShapeDtypeStruct((slab, part_width), BF16),
        ),
        in_specs=[vmem] * 6 + [hbm] * 2,
        out_specs=(hbm, hbm),
        scratch_shapes=[
            pltpu.VMEM((slab, part_width), BF16),
            pltpu.VMEM((rows, model_width), BF16),
            pltpu.VMEM((rows, model_width), BF16),
            pltpu.VMEM((rows, OWNERS * PAD), BF16),
            pltpu.VMEM((OWNERS * PAD, rows), BF16),
            pltpu.VMEM((OWNERS, SENT, block), BF16),
            pltpu.VMEM((GROUPS, OWNERS, SENT, block), BF16),
            pltpu.VMEM((GROUPS, slab, OWNERS * PAD), BF16),
            pltpu.VMEM((HALF * PAD, slab), BF16),
            pltpu.VMEM((RUNS, PARTS, BATCH, block), BF16),
            pltpu.VMEM((RUNS // 2, PARTS, BATCH, columns), BF16),
            pltpu.VMEM((GROUPS, OWNERS, SENT, columns), BF16),
            pltpu.VMEM((GROUPS, OWNERS, SENT, columns), BF16),
            pltpu.VMEM((GROUPS, OWNERS, SENT, columns), BF16),
            pltpu.VMEM((PARTS, OWNERS * PAD, columns), BF16),
            pltpu.VMEM((RUNS, PARTS, BATCH, columns), BF16),
            pltpu.VMEM((OWNERS * PAD, part_width), BF16),
            pltpu.VMEM((slab, part_width), F32),
            pltpu.VMEM((2, slab, columns), BF16),
            dma((2,)), dma((3,)), dma, dma((2,)), dma((2, GROUPS - 1)), dma((2, GROUPS - 1)),
            dma((GROUPS,)), dma((GROUPS,)), dma((GROUPS,)), dma((GROUPS,)), dma((GROUPS,)), dma((2,)),
        ],
        compiler_params=pltpu.CompilerParams(has_side_effects=True, vmem_limit_bytes=60 << 20),
        name="routed_decoder",
    )(
        (relative * PAD).astype(F32),
        block_mask.transpose(1, 2, 0),
        latent_codes.reshape(rows, 2 * slab),
        b_dec[None, :],
        jnp.asarray(order, BF16),
        jnp.asarray(order.T, BF16),
        activations,
        w_dec,
    )


def solution(mesh):
    placed = (
        P(("dp", "latent"), None),
        P(("dp", "latent"), None),
        P(("dp", "latent"), None, None),
        P(("dp", "latent"), None, None),
        P("latent", "dp"),
        P(),
    )
    return jax.shard_map(
        on_device,
        mesh=mesh,
        in_specs=placed,
        out_specs=(P(("dp", "latent"), None), P("latent", "dp")),
        check_vma=False,
    )
```

time: 477 us -> 332 us (0.70)
  Pallas kernels: 0 us -> 323 us
  blocking collectives: 239 us -> 0 us
  waiting for transfers between devices: 140 us -> 0 us
  local copies, waits for them, and re-layouts: 48.5 us -> 7.22 us
  matrix products: 33.5 us -> 0 us
  starting transfers between devices: 9.02 us -> 0 us
    pallas_call x0 -> x1, Pallas kernels: none -> 323 us  [on_device(): pl.pallas_call(kernel, out_shape=(jax.ShapeDtypeStruct((rows, model_width...]
    all_to_all x2 -> x0, blocking collectives: 239 us -> none  [the longest x1 149 us: on_device(): lax.all_to_all(error_slots.reshape(devices, MOST // 2, 2, part_width), ax...]
    all_to_all x1 -> x0, waiting for transfers between devices: 140 us -> none  [on_device(): lax.all_to_all(decoded.reshape(devices, MOST // 2, 2, part_width), axes,...]
    reshape x5 -> x0, local copies, waits for them, and re-layouts: 38.3 us -> none  [the longest x1 10.9 us: on_device(): decoded.reshape(devices, MOST // 2, 2, part_width)]
    dot_general x5 -> x0, matrix products: 33.5 us -> none  [the longest x1 11.2 us: on_device(): jnp.dot(arrived, w_dec, preferred_element_type=jnp.float32).astype(bf16)]
    all_to_all x1 -> x0, starting transfers between devices: 9.02 us -> none  [on_device(): lax.all_to_all(decoded.reshape(devices, MOST // 2, 2, part_width), axes,...]
    dot_general x1 -> x0, local copies, waits for them, and re-layouts: 8.66 us -> none  [on_device(): jnp.einsum('rs,dsj->rdj', select, returned, preferred_element_type=jnp.fl...]
    unnamed x2 -> x5, local copies, waits for them, and re-layouts: 0.01 us -> 7.22 us
  transfers between devices with their start and end apart: 1 -> 0, of which waited for: 1 -> 0; matrix products, arithmetic and copies ran while one was open for 0% -> 0% of each run, Pallas kernels for 0% -> 0%
where the time goes in v3:
time: 332 us
  Pallas kernels  323 us (97%)
  local copies, waits for them, and re-layouts  7.22 us (2%)
    pallas_call x1, Pallas kernels, on_device(): pl.pallas_call(kernel, out_shape=(jax.ShapeDtypeStruct((rows, model_width...  323 us
    unnamed x5, local copies, waits for them, and re-layouts  7.22 us

profile of v3, /device:TPU:1, one launch (start us, length us, event | category | flops | bytes accessed | tf_op | source)
XLA Modules:
  0.0 331.8 jit_solution(4536553197936683785)
XLA Ops:
  0.7 1.3 multiply_convert_fusion.rel_ref
  1.9 2.0 copy.10
  3.9 322.7 %routed_decoder.1 = (bf16[128,8192]{1,0:T(8,128)(2,1)}, bf16[1024,2048]{1,0:T(8,128)(2,1)}) custom-call(f32[2,128]{1,0:T(2,128)} %multiply_convert_fusion.rel_ref, s32[2,8,128]{2,1,0:T(8,128)} %bitcast.26, bf16[128,2048]{1,0:T(8,128)(2,1)} %bitcast.23, f32[1,8192]{1,0:T(1,128)} %bitcast.25, bf16[512,384]{1,0:T(8,128)(2,1)} %constant.85.clone.spread_ref, ...), custom_call_target="tpu_custom_call" | custom-call | tf_op jit(solution)/shard_map/routed_decoder/pallas_call | solution.py:294
  326.5 0.0 copy-start
  326.6 3.2 copy.13
  329.8 0.0 copy-done
  329.8 2.0 copy.14
Async XLA Ops:
  326.5 3.3 copy-start

commit v4 on v3

v4 whole, which is shorter than its diff:
```python
import jax
import jax.numpy as jnp
import numpy as np
from jax import lax
from jax.experimental import pallas as pl
from jax.experimental.pallas import tpu as pltpu
from jax.sharding import PartitionSpec as P

loss_scale = 1.0 / 32.0
MOST = 6
PAD = 8
PEERS = 8
PARTS = 8
GROUPS = 4
OWNERS = 64
HALF = OWNERS // 2
RUNS = OWNERS // PEERS
BATCH = PEERS * PAD
STACK = PARTS * BATCH
SENT = PARTS * MOST
BF16, F32 = jnp.bfloat16, jnp.float32
MESH = pl.DeviceIdType.MESH


def message_order():
    out = np.zeros((PARTS, PEERS, PAD, PEERS, PARTS, MOST), np.float32)
    for part in range(PARTS):
        for peer in range(PEERS):
            for slot in range(MOST):
                out[part, peer, slot, peer, part, slot] = 1
    return out.reshape(STACK, PEERS * SENT)


def dot(a, b):
    return jnp.dot(a, b, preferred_element_type=F32)


def shifted(latent, offset, sign):
    y = (latent // 16 + sign * (offset // 16) + 4) % 4
    x = (latent // 8 + offset // 8) % 2
    z = (latent % 8 + sign * (offset % 8) + 8) % 8
    return y * 16 + x * 8 + z


def bytes_wait(ref, sem):
    pltpu.make_async_copy(ref, ref, sem).wait()


def kernel(
    rel_ref, mask_ref, codes_ref, bias_hbm, spread_hbm, pack_hbm, act_hbm, w_hbm,
    rebuilt_ref, grad_ref,
    w_ref, act_ref, bias_ref, spread_ref, pack_ref, take_ref, put_ref, place_ref, used_ref, codes_out, codes_in, codes_t, codes_rows,
    term_tmp, sent, terms_in, errors_in, wide_tmp, error_tmp, total,
    load_sem, code_send, code_recv, copy_send, copy_recv, term_send, term_recv, error_send, error_recv,
):
    dp = lax.axis_index("dp")
    latent = lax.axis_index("latent")
    rows = act_ref.shape[0]
    barrier = pltpu.get_barrier_semaphore()

    def greet(ko, carry):
        pl.semaphore_signal(barrier, inc=1, device_id=(dp, shifted(latent, ko, 1)), device_id_type=MESH)
        return carry

    lax.fori_loop(1, OWNERS, greet, 0)
    for kd in range(1, GROUPS):
        pl.semaphore_signal(barrier, inc=1, device_id=((dp + kd) % GROUPS, latent), device_id_type=MESH)
    load_w = pltpu.make_async_copy(w_hbm, w_ref, load_sem.at[0])
    load_act = pltpu.make_async_copy(act_hbm, act_ref, load_sem.at[1])
    load_pack = pltpu.make_async_copy(pack_hbm, pack_ref, load_sem.at[2])
    load_spread = pltpu.make_async_copy(spread_hbm, spread_ref, load_sem.at[3])
    load_bias = pltpu.make_async_copy(bias_hbm, bias_ref, load_sem.at[4])
    load_pack.start()
    load_spread.start()
    load_w.start()
    load_bias.start()
    load_act.start()

    down = lax.broadcasted_iota(jnp.int32, (rows, rows), 0)
    across = lax.broadcasted_iota(jnp.int32, (rows, rows), 1)
    along = [jnp.broadcast_to(rel_ref[g : g + 1, :], (rows, rows)) for g in range(2)]
    below = [jnp.transpose(a) for a in along]
    slot_row = lax.broadcasted_iota(jnp.int32, (OWNERS * PAD, rows), 0).astype(F32)
    puts = []
    for g in range(2):
        count = [jnp.where(below[o] == along[g], 1.0, 0.0) for o in range(2)]
        here = rel_ref[g : g + 1, :] + jnp.sum(jnp.where(down < across, count[0] + count[1], 0.0), axis=0, keepdims=True)
        puts.append(jnp.where(slot_row == here, 1.0, 0.0))
    place_ref[...] = jnp.concatenate(puts, axis=1).astype(BF16)
    width = codes_ref.shape[1] // 2
    block = width // PARTS
    live = jnp.concatenate([mask_ref[...].astype(F32), jnp.zeros((rows - 2 * PARTS, rows), F32)], axis=0)
    live = jnp.transpose(live)
    for g in range(2):
        for part in range(PARTS):
            at = slice(part * block, (part + 1) * block)
            codes = codes_ref[:, g * width + part * block : g * width + (part + 1) * block].astype(F32)
            column = g * PARTS + part
            used_ref[g * rows : (g + 1) * rows, at] = (codes * live[:, column : column + 1]).astype(BF16)
    load_pack.wait()
    pl.semaphore_wait(barrier, OWNERS - 1 + GROUPS - 1)

    def send_codes(run, carry):
        placed = dot(place_ref[pl.ds(run * BATCH, BATCH), :], used_ref[...]).astype(BF16)
        stacked = jnp.concatenate([placed[:, part * block : (part + 1) * block] for part in range(PARTS)], axis=0)
        message = dot(pack_ref[...], stacked).astype(BF16)
        codes_out[pl.ds(run * PEERS, PEERS)] = message.reshape(PEERS, SENT, block)

        def one(i, c):
            ko = run * PEERS + i
            pltpu.make_async_remote_copy(
                codes_out.at[ko], codes_in.at[0, ko], code_send, code_recv.at[run // (RUNS // 2)],
                device_id=(dp, shifted(latent, ko, 1)), device_id_type=MESH,
            ).start()
            return c

        lax.fori_loop(jnp.where(run == 0, 1, 0), PEERS, one, 0)
        return carry

    lax.fori_loop(0, RUNS, send_codes, 0)
    pltpu.make_async_copy(codes_out.at[0], codes_in.at[0, 0], code_recv.at[0]).start()
    put_ref[...] = (puts[0] + puts[1]).astype(BF16)
    slot_lane = lax.broadcasted_iota(jnp.int32, (rows, OWNERS * PAD), 1).astype(F32)
    take = jnp.zeros((rows, OWNERS * PAD), F32)
    for g in range(2):
        count = [jnp.where(below[g] == along[o], 1.0, 0.0) for o in range(2)]
        here = below[g][:, :1] + jnp.sum(jnp.where(across < down, count[0] + count[1], 0.0), axis=1, keepdims=True)
        take = take + jnp.where(slot_lane == here, 1.0, 0.0)
    take_ref[...] = take.astype(BF16)
    unit = lax.broadcasted_iota(jnp.int32, (block, block), 0) == lax.broadcasted_iota(jnp.int32, (block, block), 1)
    unit = jnp.where(unit, 1.0, 0.0).astype(BF16)
    columns = w_ref.shape[1] // PARTS

    def forward(kd, half):
        def spread(g, carry):
            got = codes_in[kd, pl.ds(half * HALF + g * PEERS, PEERS)].reshape(PEERS * SENT, block)
            flat = dot(spread_ref[...], got).astype(BF16)
            for part in range(PARTS):
                codes_rows[pl.ds(g * BATCH, BATCH), part * block : (part + 1) * block] = flat[
                    part * BATCH : (part + 1) * BATCH
                ]
            return carry

        lax.fori_loop(0, RUNS // 2, spread, 0)

        def decode(n, carry):
            at = pl.ds(pl.multiple_of(n * columns, columns), columns)
            term = dot(codes_rows[...], w_ref[:, at]).astype(BF16)
            term_tmp[:, n] = term.reshape(RUNS // 2, BATCH, columns)
            return carry

        lax.fori_loop(0, PARTS, decode, 0)

        def pack(g, carry):
            run = half * (RUNS // 2) + g
            message = dot(pack_ref[...], term_tmp[g].reshape(STACK, columns)).astype(BF16)
            sent[kd, pl.ds(run * PEERS, PEERS)] = message.reshape(PEERS, SENT, columns)

            def one(i, c):
                ko = run * PEERS + i
                pltpu.make_async_remote_copy(
                    sent.at[kd, ko], terms_in.at[kd, ko], term_send.at[kd], term_recv.at[kd, run],
                    device_id=((dp - kd + GROUPS) % GROUPS, shifted(latent, ko, -1)), device_id_type=MESH,
                ).start()
                return c

            lax.fori_loop(jnp.where(run == 0, 1, 0) if kd == 0 else 0, PEERS, one, 0)
            return carry

        lax.fori_loop(0, RUNS // 2, pack, 0)
        for part in range(PARTS):
            turned = lax.dot_general(
                unit, codes_rows[:, part * block : (part + 1) * block], (((1,), (1,)), ((), ())),
                preferred_element_type=F32,
            )
            codes_t[kd, part * block : (part + 1) * block, half * HALF * PAD : (half + 1) * HALF * PAD] = turned.astype(BF16)

    copies = []
    for half in range(2):
        bytes_wait(codes_in.at[0, pl.ds(half * HALF, HALF)], code_recv.at[half])
        for kd in range(1, GROUPS):
            copy = pltpu.make_async_remote_copy(
                codes_in.at[0, pl.ds(half * HALF, HALF)], codes_in.at[kd, pl.ds(half * HALF, HALF)],
                copy_send.at[half, kd - 1], copy_recv.at[half, kd - 1],
                device_id=((dp + kd) % GROUPS, latent), device_id_type=MESH,
            )
            copy.start()
            copies.append((kd, half, copy))
        if half == 0:
            load_spread.wait()
            load_w.wait()
        forward(0, half)
    pltpu.make_async_copy(sent.at[0, 0], terms_in.at[0, 0], term_recv.at[0, 0]).start()
    for kd in range(1, GROUPS):
        for half in range(2):
            for ckd, chalf, copy in copies:
                if ckd == kd and chalf == half:
                    copy.wait_recv()
            forward(kd, half)
    load_act.wait()
    load_bias.wait()

    for kd in range(GROUPS):

        def spread(run, carry):
            bytes_wait(terms_in.at[kd, pl.ds(run * PEERS, PEERS)], term_recv.at[kd, run])
            got = terms_in[kd, pl.ds(run * PEERS, PEERS)].reshape(PEERS * SENT, columns)
            flat = dot(spread_ref[...], got).astype(BF16)
            wide_tmp[:, pl.ds(run * BATCH, BATCH), :] = flat.reshape(PARTS, BATCH, columns)
            return carry

        lax.fori_loop(0, RUNS, spread, 0)
        slab = (dp + kd) % GROUPS

        def combine(part, carry):
            at = pl.ds(pl.multiple_of((slab * PARTS + part) * columns, columns), columns)
            wide = dot(take_ref[...], wide_tmp[part]) + bias_ref[:, at]
            rebuilt_ref[:, at] = wide.astype(BF16)
            error = (wide - act_ref[:, at].astype(F32)).astype(BF16)
            error_tmp[:, part] = dot(put_ref[...], error).astype(BF16).reshape(RUNS, BATCH, columns)
            return carry

        lax.fori_loop(0, PARTS, combine, 0)
        bytes_wait(sent.at[kd, (1 if kd == 0 else 0) : OWNERS], term_send.at[kd])

        def pack(run, carry):
            message = dot(pack_ref[...], error_tmp[run].reshape(STACK, columns)).astype(BF16)
            sent[kd, pl.ds(run * PEERS, PEERS)] = message.reshape(PEERS, SENT, columns)

            def one(i, c):
                ko = run * PEERS + i
                pltpu.make_async_remote_copy(
                    sent.at[kd, ko], errors_in.at[kd, ko], error_send.at[kd], error_recv.at[kd, run],
                    device_id=((dp + kd) % GROUPS, shifted(latent, ko, 1)), device_id_type=MESH,
                ).start()
                return c

            lax.fori_loop(jnp.where(run == 0, 1, 0) if kd == 0 else 0, PEERS, one, 0)
            return carry

        lax.fori_loop(0, RUNS, pack, 0)
        if kd == 0:
            pltpu.make_async_copy(sent.at[0, 0], errors_in.at[0, 0], error_recv.at[0, 0]).start()

    for kd in range(GROUPS):
        for half in range(2):

            def spread(g, carry):
                run = half * (RUNS // 2) + g
                bytes_wait(errors_in.at[kd, pl.ds(run * PEERS, PEERS)], error_recv.at[kd, run])
                got = errors_in[kd, pl.ds(run * PEERS, PEERS)].reshape(PEERS * SENT, columns)
                flat = dot(spread_ref[...], got).astype(BF16)
                wide_tmp[:, pl.ds(g * BATCH, BATCH), :] = flat.reshape(PARTS, BATCH, columns)
                return carry

            lax.fori_loop(0, RUNS // 2, spread, 0)

            def accumulate(n, carry):
                at = pl.ds(pl.multiple_of(n * columns, columns), columns)
                codes = codes_t[kd, :, half * HALF * PAD : (half + 1) * HALF * PAD]
                more = dot(codes, wide_tmp[n, : HALF * PAD, :])
                if (kd, half) == (0, 0):
                    total[:, at] = more
                elif (kd, half) == (GROUPS - 1, 1):
                    grad_ref[:, at] = ((total[:, at] + more) * loss_scale).astype(BF16)
                else:
                    total[:, at] = total[:, at] + more
                return carry

            lax.fori_loop(0, PARTS, accumulate, 0)
    bytes_wait(codes_out.at[1:OWNERS], code_send)
    for _, _, copy in copies:
        copy.wait_send()
    for kd in range(GROUPS):
        bytes_wait(sent.at[kd, (1 if kd == 0 else 0) : OWNERS], error_send.at[kd])


def on_device(activations, owner_ids, block_mask, latent_codes, w_dec, b_dec):
    rows, model_width = activations.shape
    slab, part_width = w_dec.shape
    block, columns = slab // PARTS, part_width // PARTS
    latent = lax.axis_index("latent")
    owner = owner_ids.T
    relative = (
        (owner // 16 - latent // 16) % 4 * 16 + (owner // 8 - latent // 8) % 2 * 8 + (owner - latent) % 8
    )
    order = message_order()
    vmem = pl.BlockSpec(memory_space=pltpu.VMEM)
    hbm = pl.BlockSpec(memory_space=pl.ANY)
    dma = pltpu.SemaphoreType.DMA
    return pl.pallas_call(
        kernel,
        out_shape=(
            pltpu.VMEM((rows, model_width), BF16),
            pltpu.VMEM((slab, part_width), BF16),
        ),
        in_specs=[vmem] * 3 + [hbm] * 5,
        out_specs=(vmem, vmem),
        scratch_shapes=[
            pltpu.VMEM((slab, part_width), BF16),
            pltpu.VMEM((rows, model_width), BF16),
            pltpu.VMEM((1, model_width), F32),
            pltpu.VMEM((STACK, PEERS * SENT), BF16),
            pltpu.VMEM((PEERS * SENT, STACK), BF16),
            pltpu.VMEM((rows, OWNERS * PAD), BF16),
            pltpu.VMEM((OWNERS * PAD, rows), BF16),
            pltpu.VMEM((OWNERS * PAD, 2 * rows), BF16),
            pltpu.VMEM((2 * rows, slab), BF16),
            pltpu.VMEM((OWNERS, SENT, block), BF16),
            pltpu.VMEM((GROUPS, OWNERS, SENT, block), BF16),
            pltpu.VMEM((GROUPS, slab, OWNERS * PAD), BF16),
            pltpu.VMEM((HALF * PAD, slab), BF16),
            pltpu.VMEM((RUNS // 2, PARTS, BATCH, columns), BF16),
            pltpu.VMEM((GROUPS, OWNERS, SENT, columns), BF16),
            pltpu.VMEM((GROUPS, OWNERS, SENT, columns), BF16),
            pltpu.VMEM((GROUPS, OWNERS, SENT, columns), BF16),
            pltpu.VMEM((PARTS, OWNERS * PAD, columns), BF16),
            pltpu.VMEM((RUNS, PARTS, BATCH, columns), BF16),
            pltpu.VMEM((slab, part_width), F32),
            dma((5,)), dma, dma((2,)), dma((2, GROUPS - 1)), dma((2, GROUPS - 1)),
            dma((GROUPS,)), dma((GROUPS, RUNS)), dma((GROUPS,)), dma((GROUPS, RUNS)),
        ],
        compiler_params=pltpu.CompilerParams(has_side_effects=True, collective_id=0, vmem_limit_bytes=50 << 20),
        name="routed_decoder",
    )(
        (relative * PAD).astype(F32),
        block_mask.transpose(1, 2, 0).reshape(2 * PARTS, rows),
        pltpu.with_memory_space_constraint(latent_codes.reshape(rows, 2 * slab), pltpu.VMEM),
        b_dec[None, :],
        jnp.asarray(order, BF16),
        jnp.asarray(order.T, BF16),
        activations,
        w_dec,
    )


def solution(mesh):
    placed = (
        P(("dp", "latent"), None),
        P(("dp", "latent"), None),
        P(("dp", "latent"), None, None),
        P(("dp", "latent"), None, None),
        P("latent", "dp"),
        P(),
    )
    return jax.shard_map(
        on_device,
        mesh=mesh,
        in_specs=placed,
        out_specs=(P(("dp", "latent"), None), P("latent", "dp")),
        check_vma=False,
    )
```

time: 332 us -> 315 us (0.949)
  Pallas kernels: 323 us -> 309 us
    pallas_call x1, Pallas kernels: 323 us -> 309 us  [on_device(): pl.pallas_call(kernel, out_shape=(pltpu.VMEM((rows, model_width), BF16),...]
    unnamed x5 -> x3, local copies, waits for them, and re-layouts: 7.22 us -> 4.49 us
where the time goes in v4:
time: 315 us
  Pallas kernels  309 us (98%)
  local copies, waits for them, and re-layouts  4.49 us (1%)
    pallas_call x1, Pallas kernels, on_device(): pl.pallas_call(kernel, out_shape=(pltpu.VMEM((rows, model_width), BF16),...  309 us

profile of v4, /device:TPU:1, one launch (start us, length us, event | category | flops | bytes accessed | tf_op | source)
XLA Modules:
  0.0 315.1 jit_solution(324755180987760574)
XLA Ops:
  0.7 1.3 multiply_convert_fusion.rel_ref
  1.9 1.2 copy.10
  3.1 308.6 %routed_decoder.1 = (bf16[128,8192]{1,0:T(8,128)(2,1)S(1)}, bf16[1024,2048]{1,0:T(8,128)(2,1)S(1)}) custom-call(f32[2,128]{1,0:T(2,128)} %multiply_convert_fusion.rel_ref, s32[16,128]{1,0:T(8,128)} %bitcast.28, bf16[128,2048]{1,0:T(8,128)(2,1)S(1)} %bitcast.25, f32[1,8192]{1,0:T(1,128)} %bitcast.27, bf16[512,384]{1,0:T(8,128)(2,1)} %constant.85.clone.spread_hbm, ...), custom_call_target="tpu_custom_call" | custom-call | tf_op jit(solution)/shard_map/routed_decoder/pallas_call | solution.py:291
  311.7 1.3 copy.13
  313.1 2.0 copy.14

commit v5 on v4

--- a/solution.py
+++ b/solution.py
@@ -42,16 +42,37 @@
     return y * 16 + x * 8 + z
 
 
+def relay_step(z_offset, y_offset):
+    ahead = jnp.where(z_offset + y_offset % 2 <= 4, 1, -1)
+    return jnp.where(z_offset == 0, 0, ahead)
+
+
+def relayed(latent, offset, sign):
+    y = (latent // 16 + sign * (offset // 16) + 4) % 4
+    x = (latent // 8 + offset // 8) % 2
+    z = (latent % 8 + sign * (offset % 8 - relay_step(offset % 8, offset // 16)) + 16) % 8
+    return y * 16 + x * 8 + z
+
+
+def relay_roles(rows):
+    out = np.zeros((OWNERS, PAD, rows), np.float32)
+    for offset in range(OWNERS):
+        if offset % 8:
+            out[offset] = 1 if offset % 8 + offset // 16 % 2 <= 4 else 2
+    return out.reshape(OWNERS * PAD, rows)
+
+
 def bytes_wait(ref, sem):
     pltpu.make_async_copy(ref, ref, sem).wait()
 
 
 def kernel(
-    rel_ref, mask_ref, codes_ref, bias_hbm, spread_hbm, pack_hbm, act_hbm, w_hbm,
+    rel_ref, mask_ref, codes_ref, bias_hbm, spread_hbm, pack_hbm, roles_hbm, act_hbm, w_hbm,
     rebuilt_ref, grad_ref,
-    w_ref, act_ref, bias_ref, spread_ref, pack_ref, take_ref, put_ref, place_ref, used_ref, codes_out, codes_in, codes_t, codes_rows,
-    term_tmp, sent, terms_in, errors_in, wide_tmp, error_tmp, total,
+    w_ref, act_ref, bias_ref, spread_ref, pack_ref, roles_ref, take_ref, put_ref, place_ref, used_ref, codes_out, codes_in, codes_t, codes_rows,
+    slot_out, slot_in, error_all, sent, terms_in, errors_in, wide_tmp, error_tmp, total,
     load_sem, code_send, code_recv, copy_send, copy_recv, term_send, term_recv, error_send, error_recv,
+    slot_send, slot_recv, row_send, row_recv,
 ):
     dp = lax.axis_index("dp")
     latent = lax.axis_index("latent")
@@ -70,7 +91,9 @@
     load_pack = pltpu.make_async_copy(pack_hbm, pack_ref, load_sem.at[2])
     load_spread = pltpu.make_async_copy(spread_hbm, spread_ref, load_sem.at[3])
     load_bias = pltpu.make_async_copy(bias_hbm, bias_ref, load_sem.at[4])
+    load_roles = pltpu.make_async_copy(roles_hbm, roles_ref, load_sem.at[5])
     load_pack.start()
+    load_roles.start()
     load_spread.start()
     load_w.start()
     load_bias.start()
@@ -81,10 +104,12 @@
     along = [jnp.broadcast_to(rel_ref[g : g + 1, :], (rows, rows)) for g in range(2)]
     below = [jnp.transpose(a) for a in along]
     slot_row = lax.broadcasted_iota(jnp.int32, (OWNERS * PAD, rows), 0).astype(F32)
+    slot_out[...] = jnp.zeros_like(slot_out)
     puts = []
     for g in range(2):
         count = [jnp.where(below[o] == along[g], 1.0, 0.0) for o in range(2)]
         here = rel_ref[g : g + 1, :] + jnp.sum(jnp.where(down < across, count[0] + count[1], 0.0), axis=0, keepdims=True)
+        slot_out[g : g + 1, :] = here
         puts.append(jnp.where(slot_row == here, 1.0, 0.0))
     place_ref[...] = jnp.concatenate(puts, axis=1).astype(BF16)
     width = codes_ref.shape[1] // 2
@@ -99,6 +124,16 @@
             used_ref[g * rows : (g + 1) * rows, at] = (codes * live[:, column : column + 1]).astype(BF16)
     load_pack.wait()
     pl.semaphore_wait(barrier, OWNERS - 1 + GROUPS - 1)
+    beside = [(dp, shifted(latent, 1, -1)), (dp, shifted(latent, 1, 1))]
+
+    def to_side(side, source, target, send, recv):
+        return pltpu.make_async_remote_copy(
+            source, target, send, recv, device_id=beside[side], device_id_type=MESH
+        )
+
+    slot_copies = [to_side(i, slot_out, slot_in.at[1 - i], slot_send.at[i], slot_recv.at[1 - i]) for i in range(2)]
+    for copy in slot_copies:
+        copy.start()
 
     def send_codes(run, carry):
         placed = dot(place_ref[pl.ds(run * BATCH, BATCH), :], used_ref[...]).astype(BF16)
@@ -119,14 +154,18 @@
 
     lax.fori_loop(0, RUNS, send_codes, 0)
     pltpu.make_async_copy(codes_out.at[0], codes_in.at[0, 0], code_recv.at[0]).start()
-    put_ref[...] = (puts[0] + puts[1]).astype(BF16)
-    slot_lane = lax.broadcasted_iota(jnp.int32, (rows, OWNERS * PAD), 1).astype(F32)
-    take = jnp.zeros((rows, OWNERS * PAD), F32)
-    for g in range(2):
-        count = [jnp.where(below[g] == along[o], 1.0, 0.0) for o in range(2)]
-        here = below[g][:, :1] + jnp.sum(jnp.where(across < down, count[0] + count[1], 0.0), axis=1, keepdims=True)
-        take = take + jnp.where(slot_lane == here, 1.0, 0.0)
-    take_ref[...] = take.astype(BF16)
+    load_roles.wait()
+    for role in range(3):
+        if role:
+            bytes_wait(slot_in.at[role - 1], slot_recv.at[role - 1])
+        put = jnp.zeros((OWNERS * PAD, rows), F32)
+        for g in range(2):
+            where = slot_in[role - 1, g : g + 1, :] if role else slot_out[g : g + 1, :]
+            put = put + jnp.where(slot_row == where, 1.0, 0.0)
+        if role == 0:
+            take_ref[...] = jnp.transpose(put).astype(BF16)
+        put = jnp.where(roles_ref[...] == float(role), put, 0.0)
+        put_ref[:, role * rows : (role + 1) * rows] = put.astype(BF16)
     unit = lax.broadcasted_iota(jnp.int32, (block, block), 0) == lax.broadcasted_iota(jnp.int32, (block, block), 1)
     unit = jnp.where(unit, 1.0, 0.0).astype(BF16)
     columns = w_ref.shape[1] // PARTS
@@ -146,14 +185,14 @@
         def decode(n, carry):
             at = pl.ds(pl.multiple_of(n * columns, columns), columns)
             term = dot(codes_rows[...], w_ref[:, at]).astype(BF16)
-            term_tmp[:, n] = term.reshape(RUNS // 2, BATCH, columns)
+            error_tmp[: RUNS // 2, n] = term.reshape(RUNS // 2, BATCH, columns)
             return carry
 
         lax.fori_loop(0, PARTS, decode, 0)
 
         def pack(g, carry):
             run = half * (RUNS // 2) + g
-            message = dot(pack_ref[...], term_tmp[g].reshape(STACK, columns)).astype(BF16)
+            message = dot(pack_ref[...], error_tmp[g].reshape(STACK, columns)).astype(BF16)
             sent[kd, pl.ds(run * PEERS, PEERS)] = message.reshape(PEERS, SENT, columns)
 
             def one(i, c):
@@ -191,17 +230,20 @@
             load_w.wait()
         forward(0, half)
     pltpu.make_async_copy(sent.at[0, 0], terms_in.at[0, 0], term_recv.at[0, 0]).start()
-    for kd in range(1, GROUPS):
+
+    def decode_for(kd):
         for half in range(2):
             for ckd, chalf, copy in copies:
                 if ckd == kd and chalf == half:
                     copy.wait_recv()
             forward(kd, half)
+
+    for kd in range(1, GROUPS):
+        decode_for(kd)
     load_act.wait()
     load_bias.wait()
 
-    for kd in range(GROUPS):
-
+    def compare(kd):
         def spread(run, carry):
             bytes_wait(terms_in.at[kd, pl.ds(run * PEERS, PEERS)], term_recv.at[kd, run])
             got = terms_in[kd, pl.ds(run * PEERS, PEERS)].reshape(PEERS * SENT, columns)
@@ -216,11 +258,28 @@
             at = pl.ds(pl.multiple_of((slab * PARTS + part) * columns, columns), columns)
             wide = dot(take_ref[...], wide_tmp[part]) + bias_ref[:, at]
             rebuilt_ref[:, at] = wide.astype(BF16)
-            error = (wide - act_ref[:, at].astype(F32)).astype(BF16)
-            error_tmp[:, part] = dot(put_ref[...], error).astype(BF16).reshape(RUNS, BATCH, columns)
+            error_all[kd, part, :rows] = (wide - act_ref[:, at].astype(F32)).astype(BF16)
+            for side in range(2):
+                first = (2 - side) * rows
+                to_side(
+                    side, error_all.at[kd, part, :rows], error_all.at[kd, part, first : first + rows],
+                    row_send.at[kd, side], row_recv.at[kd, 1 - side],
+                ).start()
             return carry
 
         lax.fori_loop(0, PARTS, combine, 0)
+
+    def scatter(kd):
+        for side in range(2):
+            first = (1 + side) * rows
+            bytes_wait(error_all.at[kd, :, first : first + rows], row_recv.at[kd, side])
+
+        def place(part, carry):
+            placed = dot(put_ref[...], error_all[kd, part]).astype(BF16)
+            error_tmp[:, part] = placed.reshape(RUNS, BATCH, columns)
+            return carry
+
+        lax.fori_loop(0, PARTS, place, 0)
         bytes_wait(sent.at[kd, (1 if kd == 0 else 0) : OWNERS], term_send.at[kd])
 
         def pack(run, carry):
@@ -231,16 +290,24 @@
                 ko = run * PEERS + i
                 pltpu.make_async_remote_copy(
                     sent.at[kd, ko], errors_in.at[kd, ko], error_send.at[kd], error_recv.at[kd, run],
-                    device_id=((dp + kd) % GROUPS, shifted(latent, ko, 1)), device_id_type=MESH,
+                    device_id=((dp + kd) % GROUPS, relayed(latent, ko, 1)), device_id_type=MESH,
                 ).start()
                 return c
 
-            lax.fori_loop(jnp.where(run == 0, 1, 0) if kd == 0 else 0, PEERS, one, 0)
+            bounds = (jnp.where(run == 0, 2, 0), jnp.where(run == 0, PEERS - 1, PEERS)) if kd == 0 else (0, PEERS)
+            lax.fori_loop(*bounds, one, 0)
             return carry
 
         lax.fori_loop(0, RUNS, pack, 0)
         if kd == 0:
-            pltpu.make_async_copy(sent.at[0, 0], errors_in.at[0, 0], error_recv.at[0, 0]).start()
+            for ko in (0, 1, PEERS - 1):
+                pltpu.make_async_copy(sent.at[0, ko], errors_in.at[0, ko], error_recv.at[0, 0]).start()
+
+    compare(0)
+    for kd in range(GROUPS):
+        if kd < GROUPS - 1:
+            compare(kd + 1)
+        scatter(kd)
 
     for kd in range(GROUPS):
         for half in range(2):
@@ -272,7 +339,12 @@
     for _, _, copy in copies:
         copy.wait_send()
     for kd in range(GROUPS):
-        bytes_wait(sent.at[kd, (1 if kd == 0 else 0) : OWNERS], error_send.at[kd])
+        bytes_wait(sent.at[kd, (3 if kd == 0 else 0) : OWNERS], error_send.at[kd])
+    for copy in slot_copies:
+        copy.wait_send()
+    for kd in range(GROUPS):
+        for side in range(2):
+            bytes_wait(error_all.at[kd, :, :rows], row_send.at[kd, side])
 
 
 def on_device(activations, owner_ids, block_mask, latent_codes, w_dec, b_dec):
@@ -294,7 +366,7 @@
             pltpu.VMEM((rows, model_width), BF16),
             pltpu.VMEM((slab, part_width), BF16),
         ),
-        in_specs=[vmem] * 3 + [hbm] * 5,
+        in_specs=[vmem] * 3 + [hbm] * 6,
         out_specs=(vmem, vmem),
         scratch_shapes=[
             pltpu.VMEM((slab, part_width), BF16),
@@ -302,25 +374,29 @@
             pltpu.VMEM((1, model_width), F32),
             pltpu.VMEM((STACK, PEERS * SENT), BF16),
             pltpu.VMEM((PEERS * SENT, STACK), BF16),
+            pltpu.VMEM((OWNERS * PAD, rows), F32),
             pltpu.VMEM((rows, OWNERS * PAD), BF16),
-            pltpu.VMEM((OWNERS * PAD, rows), BF16),
+            pltpu.VMEM((OWNERS * PAD, 3 * rows), BF16),
             pltpu.VMEM((OWNERS * PAD, 2 * rows), BF16),
             pltpu.VMEM((2 * rows, slab), BF16),
             pltpu.VMEM((OWNERS, SENT, block), BF16),
             pltpu.VMEM((GROUPS, OWNERS, SENT, block), BF16),
             pltpu.VMEM((GROUPS, slab, OWNERS * PAD), BF16),
             pltpu.VMEM((HALF * PAD, slab), BF16),
-            pltpu.VMEM((RUNS // 2, PARTS, BATCH, columns), BF16),
+            pltpu.VMEM((8, rows), F32),
+            pltpu.VMEM((2, 8, rows), F32),
+            pltpu.VMEM((GROUPS, PARTS, 3 * rows, columns), BF16),
             pltpu.VMEM((GROUPS, OWNERS, SENT, columns), BF16),
             pltpu.VMEM((GROUPS, OWNERS, SENT, columns), BF16),
             pltpu.VMEM((GROUPS, OWNERS, SENT, columns), BF16),
             pltpu.VMEM((PARTS, OWNERS * PAD, columns), BF16),
             pltpu.VMEM((RUNS, PARTS, BATCH, columns), BF16),
             pltpu.VMEM((slab, part_width), F32),
-            dma((5,)), dma, dma((2,)), dma((2, GROUPS - 1)), dma((2, GROUPS - 1)),
+            dma((6,)), dma, dma((2,)), dma((2, GROUPS - 1)), dma((2, GROUPS - 1)),
             dma((GROUPS,)), dma((GROUPS, RUNS)), dma((GROUPS,)), dma((GROUPS, RUNS)),
+            dma((2,)), dma((2,)), dma((GROUPS, 2)), dma((GROUPS, 2)),
         ],
-        compiler_params=pltpu.CompilerParams(has_side_effects=True, collective_id=0, vmem_limit_bytes=50 << 20),
+        compiler_params=pltpu.CompilerParams(has_side_effects=True, collective_id=0, vmem_limit_bytes=57 << 20),
         name="routed_decoder",
     )(
         (relative * PAD).astype(F32),
@@ -329,6 +405,7 @@
         b_dec[None, :],
         jnp.asarray(order, BF16),
         jnp.asarray(order.T, BF16),
+        jnp.asarray(relay_roles(rows)),
         activations,
         w_dec,
     )

time: 315 us -> 303 us (0.962)
  Pallas kernels: 309 us -> 297 us
    pallas_call x1, Pallas kernels: 309 us -> 297 us  [on_device(): pl.pallas_call(kernel, out_shape=(pltpu.VMEM((rows, model_width), BF16),...]
where the time goes in v5:
time: 303 us
  Pallas kernels  297 us (98%)
  local copies, waits for them, and re-layouts  4.49 us (1%)
    pallas_call x1, Pallas kernels, on_device(): pl.pallas_call(kernel, out_shape=(pltpu.VMEM((rows, model_width), BF16),...  297 us

profile of v5, /device:TPU:1, one launch (start us, length us, event | category | flops | bytes accessed | tf_op | source)
XLA Modules:
  0.0 303.1 jit_solution(2619346309055373489)
XLA Ops:
  0.7 1.3 multiply_convert_fusion.rel_ref
  1.9 1.2 copy.11
  3.1 296.7 %routed_decoder.1 = (bf16[128,8192]{1,0:T(8,128)(2,1)S(1)}, bf16[1024,2048]{1,0:T(8,128)(2,1)S(1)}) custom-call(f32[2,128]{1,0:T(2,128)} %multiply_convert_fusion.rel_ref, s32[16,128]{1,0:T(8,128)} %bitcast.28, bf16[128,2048]{1,0:T(8,128)(2,1)S(1)} %bitcast.25, f32[1,8192]{1,0:T(1,128)} %bitcast.27, bf16[512,384]{1,0:T(8,128)(2,1)} %constant.87.clone.spread_hbm, ...), custom_call_target="tpu_custom_call" | custom-call | tf_op jit(solution)/shard_map/routed_decoder/pallas_call | solution.py:363
  299.8 1.3 copy.14
  301.1 2.0 copy.15
